TPU v7x, 32 devices: a whole 2x2x4 slice. The times are simulated.
32 devices in a mesh: branch: 2 (over core), dap: 4 (over z), rep: 4 (over y, x).
Axes of the slice: x: 2, y: 2, z: 4, core: 2. Of those that a mesh axis runs over, the one named last changes fastest.
Arguments:
- homolog_stack: bfloat16 [512, 32, 256], P(('rep', 'branch', 'dap')), parts along dimension 0, may hold values from -6 to 6
- homolog_validity_flags: int32 [512], P(('rep', 'branch', 'dap')), parts along dimension 0, may hold values 0 or 1
- amino_validity_flags: int32 [128], P('rep'), parts along dimension 0, may hold values from 0 to 1, as said below
- offset_classes: int32 [128, 32], P(('rep', 'branch', 'dap')), parts along dimension 0, may hold values from 0 to 65
- couple_matrix: bfloat16 [128, 32, 128], P(('rep', 'branch', 'dap')), parts along dimension 0, may hold values from -6 to 6
- homolog_standardizer_factor: float32 [256], replicated, may hold values from 0.25 to 1.75
- first_factor_projector: bfloat16 [256, 32], replicated, may hold values from -0.375 to 0.375
- second_factor_projector: bfloat16 [256, 32], replicated, may hold values from -0.375 to 0.375
- product_final_projector: bfloat16 [1024, 128], replicated, may hold values from -0.1875 to 0.1875
- offset_embedding_matrix: bfloat16 [66, 128], replicated, may hold values from -6 to 6
- couple_standardizer_factor: float32 [128], replicated, may hold values from 0.25 to 1.75
- trilateral_edge_projectors: bfloat16 [128, 512], replicated, may hold values from -0.5 to 0.5
- trilateral_sigmoid_projector: bfloat16 [128, 128], replicated, may hold values from -0.5 to 0.5
- trilateral_final_projector: bfloat16 [128, 128], replicated, may hold values from -0.5 to 0.5
- trilateral_standardizer_factor: float32 [128], replicated, may hold values from 0.25 to 1.75
Outputs:
- pair_out: bfloat16 [128, 32, 128], P(('rep', 'branch', 'dap')), parts along dimension 0
There are 4 independent parts, one for each index of `rep`. A program takes and returns all parts, laid end to end along the dimension named above; an argument that names none is the same for every part. Nothing has to cross between parts.
Inputs may be any that keep to these rules, and one draw needn't show every extreme that they name: `amino_validity_flags`: 0 or 1; exactly 12 residues are 0, at any positions.
All inputs are finite; a program needn't handle non-finite values. No bound on the sum of `homolog_validity_flags` on one device may be relied on, other than what follows from the above.
Results may differ from a plain program's by a relative error of at most 0.0036.
Values may be sent and summed in bfloat16 or wider, within the bound.
A program may use at most 64 MiB of HBM per device.

v0:
```python
import functools

import jax
import jax.numpy as jnp
from jax import lax
from jax.experimental import pallas as pl
from jax.experimental.pallas import tpu as pltpu
from jax.sharding import PartitionSpec as P

F32 = jnp.float32
BF16 = jnp.bfloat16
MESH = pl.DeviceIdType.MESH
OPERANDS = 15
LANES = 128
SUB = 8


def iota(shape, axis):
    return lax.broadcasted_iota(jnp.int32, shape, axis)


def dot(a, b):
    return jnp.dot(a, b, preferred_element_type=F32)


def standardize(values, gain):
    mean = jnp.mean(values, axis=-1, keepdims=True)
    centred = values - mean
    spread = jnp.mean(centred * centred, axis=-1, keepdims=True)
    return centred * lax.rsqrt(spread + 1e-05) * gain


def kernel(
    nb, nz,
    *refs,
):
    operands, out_ref, held = refs[:OPERANDS], refs[OPERANDS], refs[OPERANDS + 1 : 2 * OPERANDS + 1]
    in_sem, *scratch = refs[2 * OPERANDS + 1 :]
    (x_ref, hflag_ref, aflag_ref, class_ref, couple_ref, hgain_ref, wl_ref, wr_ref, wout_ref,
     embed_ref, cgain_ref, wedge_ref, wgate_ref, wfin_ref, tgain_ref) = held
    (
    flag_all, right_all, left_send, left_all, tri_all, y_left, outer_buf, w_wide, w_perm, tri_buf,
    flag_ssem, flag_rsem, right_ssem, right_rsem, right_fsem, left_ssem, left_rsem,
    tri_ssem, tri_rsem, tri_fsem,
    ) = scratch
    n = nb * nz
    branch = lax.axis_index("branch")
    dap = lax.axis_index("dap")
    me = branch * nz + dap
    amino = aflag_ref.shape[1]
    seqs = hflag_ref.shape[1]
    rows = class_ref.shape[0]
    inner = wl_ref.shape[0]
    width = couple_ref.shape[1]
    reps = LANES // inner
    live = amino - 3 * amino // 8
    groups = live // reps
    pairs = rows * amino
    padded = -(-live // SUB) * SUB
    first = me * rows

    same = [(branch, lax.rem(dap + step, nz)) for step in range(1, nz)]
    here = [(lax.rem(branch + step, nb), dap) for step in range(1, nb)]
    far = [(b[0], z[1]) for b in here for z in same]
    near = same + here
    everyone = near + far

    def index_of(peer):
        return peer[0] * nz + peer[1]

    def target(peer):
        return {"branch": peer[0], "dap": peer[1]}

    barrier = pltpu.get_barrier_semaphore()
    for peer in everyone:
        pl.semaphore_signal(barrier, inc=1, device_id=target(peer), device_id_type=MESH)

    loads = {}
    for k in (2, 1, 0, 5, 6, 7, 8, 3, 4, 9, 10, 11, 12, 13, 14):
        loads[k] = pltpu.make_async_copy(operands[k], held[k], in_sem.at[k])
        loads[k].start()

    loads[2].wait()
    loads[1].wait()
    aflag = jnp.broadcast_to(aflag_ref[...].astype(F32), (SUB, amino)).astype(BF16)
    hflag32 = hflag_ref[...].astype(F32)
    hflag = jnp.broadcast_to(hflag32, (SUB, seqs)).astype(BF16)

    def lane_keys(lanes):
        r = iota((amino, lanes), 0)
        k = lax.rem(iota((amino, lanes), 1), amino)
        count = dot(aflag, (r <= k).astype(BF16))
        alive = dot(aflag, (r == k).astype(BF16))
        return (count * alive)[0:1, :]

    flag_all[me] = jnp.broadcast_to(jnp.sum(hflag32, axis=1, keepdims=True), (1, LANES))

    total = seqs * amino
    key_x = lane_keys(total)
    hlane = dot(hflag, (iota((seqs, total), 0) == iota((seqs, total), 1) // amino).astype(BF16))[0:1, :]
    key_x = jnp.where(hlane > 0.5, key_x, 0.0).astype(jnp.int32)
    m_row = iota((live * seqs, 1), 0)
    same_seq = lax.rem(m_row, seqs) == iota((1, total), 1) // amino
    gather_right = jnp.where((key_x == m_row // seqs + 1) & same_seq, 1.0, 0.0).astype(BF16)
    lane_group = iota((1, LANES), 1) // inner
    alane = dot(
        aflag,
        (iota((amino, amino * inner), 0) == iota((amino, amino * inner), 1) // inner).astype(BF16),
    )[0:1, :]

    for k in (0, 5, 6, 7):
        loads[k].wait()
    normed = standardize(x_ref[...].astype(F32), hgain_ref[...]).astype(BF16)
    w_both = jnp.concatenate([wl_ref[...]] * reps + [wr_ref[...]] * reps, axis=0)
    sides = lax.dot_general(
        normed, w_both, (((1,), (1,)), ((), ())), preferred_element_type=F32
    )
    y_left[...] = sides[:, :LANES]
    right_rows = dot(gather_right, sides[:, LANES:].astype(BF16))
    for q in range(groups):
        block = right_rows[q * reps * seqs : (q * reps + 1) * seqs]
        for g in range(1, reps):
            start = (q * reps + g) * seqs
            block = jnp.where(lane_group == g, right_rows[start : start + seqs], block)
        right_all[me, :, q * LANES : (q + 1) * LANES] = block.astype(BF16)
    for d in range(n):
        block = y_left[pl.ds(d * rows, seqs, stride=amino), :]
        for g in range(1, rows):
            block = jnp.where(
                lane_group == g, y_left[pl.ds(d * rows + g, seqs, stride=amino), :], block
            )
        left_send[d] = (block * alane[:, d * LANES : (d + 1) * LANES]).astype(BF16)

    pl.semaphore_wait(barrier, n - 1)

    sends = []

    def push(src, dst, ssem, rsem, peer):
        copy = pltpu.make_async_remote_copy(
            src_ref=src, dst_ref=dst, send_sem=ssem, recv_sem=rsem,
            device_id=target(peer), device_id_type=MESH,
        )
        copy.start()
        sends.append(copy)

    def arrived(ref, slot, rsem):
        pltpu.make_async_remote_copy(
            src_ref=ref.at[slot], dst_ref=ref.at[slot], send_sem=rsem.at[slot],
            recv_sem=rsem.at[slot], device_id=target(everyone[0]), device_id_type=MESH,
        ).wait_recv()

    for peer in everyone:
        d = index_of(peer)
        push(flag_all.at[me], flag_all.at[me], flag_ssem.at[d], flag_rsem.at[me], peer)
    for peer in near:
        push(right_all.at[me], right_all.at[me], right_ssem.at[index_of(peer)], right_rsem.at[me], peer)
    for peer in everyone:
        d = index_of(peer)
        push(left_send.at[d], left_all.at[me], left_ssem.at[d], left_rsem.at[me], peer)
    left_all[me] = left_send[me]

    for k in (8, 3, 4, 9, 10, 11, 12, 13, 14):
        loads[k].wait()
    w_wide[...] = wout_ref[...].astype(F32)
    for e in range(inner):
        w_perm[e * inner : (e + 1) * inner, :] = w_wide[
            pl.ds(e, inner, stride=inner), :
        ].astype(BF16)
    eye = iota((amino, amino), 0) == iota((amino, amino), 1)
    bins = embed_ref.shape[0]
    hot = []
    for i in range(rows):
        column = jnp.sum(
            jnp.where(eye, class_ref[i : i + 1, :], 0).astype(F32), axis=1, keepdims=True
        ).astype(jnp.int32)
        hot.append(jnp.where(column == iota((amino, bins), 1), 1.0, 0.0))
    onehot = jnp.concatenate(hot, axis=0).astype(BF16)
    base = couple_ref[...].astype(F32) + dot(onehot, embed_ref[...])

    key_pair = lane_keys(pairs)
    ilane = dot(
        aflag, (iota((amino, pairs), 0) == first + iota((amino, pairs), 1) // amino).astype(BF16)
    )[0:1, :]
    key_pair = jnp.where(ilane > 0.5, key_pair, 0.0).astype(jnp.int32)
    pair_row = iota((1, pairs), 1) // amino
    sel_rows = live * rows
    sel_m = iota((sel_rows, 1), 0)
    sel_key = key_pair == sel_m // rows + 1
    select_right = jnp.where(sel_key & (pair_row == lax.rem(sel_m, rows)), 1.0, 0.0).astype(BF16)
    select_left = jnp.concatenate(
        [jnp.where(sel_key & (pair_row == i), 1.0, 0.0) for i in range(rows)], axis=0
    ).astype(BF16)
    wide_key = jnp.broadcast_to(lane_keys(amino), (amino, amino))
    key_col = jnp.sum(jnp.where(eye, wide_key, 0.0), axis=1, keepdims=True).astype(jnp.int32)
    key_col = jnp.concatenate([key_col] * rows, axis=0)
    slots = rows * padded
    col = iota((pairs, slots), 1)
    expand = jnp.where(
        (key_col == lax.rem(col, padded) + 1) & (iota((pairs, slots), 0) // amino == col // padded),
        1.0,
        0.0,
    ).astype(BF16)
    expand = jnp.concatenate([expand, expand], axis=1)
    if padded > live:
        outer_buf[live * inner :, :] = jnp.zeros(((padded - live) * inner, LANES), F32)

    for peer in same:
        slot = index_of(peer)
        arrived(right_all, slot, right_rsem)
        for k, other in enumerate(here):
            push(right_all.at[slot], right_all.at[slot], right_fsem.at[k, peer[1]], right_rsem.at[slot], other)
    for peer in everyone:
        arrived(left_all, index_of(peer), left_rsem)
        arrived(flag_all, index_of(peer), flag_rsem)
    for peer in here + far:
        arrived(right_all, index_of(peer), right_rsem)

    number = jnp.maximum(jnp.sum(flag_all[...], axis=0), 1.0)
    left = left_all[...].reshape(n * seqs, LANES)
    right = right_all[...].reshape(n * seqs, live * inner)
    outer_buf[: live * inner, :] = lax.dot_general(
        right, left, (((0,), (0,)), ((), ())), preferred_element_type=F32
    )
    parts = [[] for _ in range(rows)]
    lane = iota((1, LANES), 1)
    for q in range(inner // reps):
        block = [outer_buf[pl.ds(q * reps + g, padded, stride=inner), :] for g in range(reps)]
        span = reps // 2
        while span:
            upper = (lane // (span * inner)) % 2 == 1
            new = list(block)
            for a in range(reps):
                if a & span:
                    continue
                b = a | span
                shift = span * inner
                new[a] = jnp.where(upper, pltpu.roll(block[b], shift, 1), block[a])
                new[b] = jnp.where(upper, block[b], pltpu.roll(block[a], LANES - shift, 1))
            block = new
            span //= 2
        for i in range(rows):
            parts[i].append(block[i])
    packed = jnp.concatenate([jnp.concatenate(p, axis=1) for p in parts], axis=0).astype(BF16)
    product = dot(packed, w_perm[...])
    high = product.astype(BF16)
    low = (product - high.astype(F32)).astype(BF16)
    projected = dot(expand, jnp.concatenate([high, low], axis=0))
    updated = base + projected / number
    pair = standardize(updated, cgain_ref[...]).astype(BF16)
    right_two = dot(pair, wedge_ref[:, 2 * width :])
    tri_right = (jax.nn.sigmoid(right_two[:, :width]) * right_two[:, width:]).astype(BF16)
    tri_all[me] = dot(select_right, tri_right).astype(BF16)
    for peer in near:
        push(tri_all.at[me], tri_all.at[me], tri_ssem.at[index_of(peer)], tri_rsem.at[me], peer)

    left_two = dot(pair, wedge_ref[:, : 2 * width])
    tri_left = (jax.nn.sigmoid(left_two[:, :width]) * left_two[:, width:]).astype(BF16)
    spread_left = dot(select_left, tri_left)
    gate = jax.nn.sigmoid(dot(pair, wgate_ref[...]))

    def passing(peer):
        slot = index_of(peer)
        arrived(tri_all, slot, tri_rsem)
        for k, other in enumerate(here):
            push(tri_all.at[slot], tri_all.at[slot], tri_fsem.at[k, peer[1]], tri_rsem.at[slot], other)

    pieces = SUB // rows
    sub = iota((SUB, LANES), 0)

    def triangle(start):
        blocks = [tri_all[start + h].astype(F32) for h in range(pieces)]
        for i in range(rows):
            mine = spread_left[i * sel_rows : (i + 1) * sel_rows]
            result = None
            for h in range(pieces):
                both = mine * blocks[h]
                acc = jnp.sum(both.reshape(sel_rows // SUB, SUB, LANES), axis=0)
                step = rows
                while step < SUB:
                    acc = acc + pltpu.roll(acc, step, 0)
                    step *= 2
                result = acc if result is None else jnp.where(sub // rows == h, acc, result)
            row = i * amino + start * rows
            tri_buf[pl.ds(row if isinstance(row, int) else pl.multiple_of(row, SUB), SUB), :] = result

    for peer in same:
        passing(peer)
    if nz % pieces == 0:
        for b in [branch] + [o[0] for o in here]:
            if b is not branch:
                for peer in here + far:
                    if peer[0] is b:
                        arrived(tri_all, index_of(peer), tri_rsem)
            for z in range(0, nz, pieces):
                triangle(b * nz + z)
    else:
        for peer in here + far:
            arrived(tri_all, index_of(peer), tri_rsem)
        for d in range(0, n, pieces):
            triangle(d)
    tri = standardize(tri_buf[...], tgain_ref[...]).astype(BF16)
    out_ref[...] = (updated + gate * dot(tri, wfin_ref[...])).astype(BF16)
    for copy in sends:
        copy.wait_send()


def on_device(nb, nz, x, hflags, aflags, classes, couple, hgain, wl, wr, wout, embed, cgain, wedge, wgate, wfin, tgain):
    n = nb * nz
    seqs, amino, depth = x.shape
    rows, _, width = couple.shape
    inner = wl.shape[1]
    live = amino - 3 * amino // 8
    padded = -(-live // SUB) * SUB
    dma = pltpu.SemaphoreType.DMA
    operands = (
        x.reshape(seqs * amino, depth), hflags.reshape(1, seqs), aflags.reshape(1, amino), classes,
        couple.reshape(rows * amino, width), hgain.reshape(1, depth), wl.T, wr.T, wout, embed,
        cgain.reshape(1, width), wedge, wgate, wfin, tgain.reshape(1, width),
    )
    out = pl.pallas_call(
        functools.partial(kernel, nb, nz),
        out_shape=pltpu.VMEM((rows * amino, width), BF16),
        in_specs=[pl.BlockSpec(memory_space=pl.ANY)] * OPERANDS,
        out_specs=pl.BlockSpec(memory_space=pltpu.VMEM),
        scratch_shapes=[pltpu.VMEM(a.shape, a.dtype) for a in operands]
        + [
            dma((OPERANDS,)),
            pltpu.VMEM((n, 1, LANES), F32),
            pltpu.VMEM((n, seqs, live * inner), BF16),
            pltpu.VMEM((n, seqs, LANES), BF16),
            pltpu.VMEM((n, seqs, LANES), BF16),
            pltpu.VMEM((n, live * rows, width), BF16),
            pltpu.VMEM((seqs * amino, LANES), F32),
            pltpu.VMEM((padded * inner, LANES), F32),
            pltpu.VMEM((inner * inner, width), F32),
            pltpu.VMEM((inner * inner, width), BF16),
            pltpu.VMEM((rows * amino, width), F32),
            dma((n,)), dma((n,)),
            dma((n,)), dma((n,)), dma((nb, nz)),
            dma((n,)), dma((n,)),
            dma((n,)), dma((n,)), dma((nb, nz)),
        ],
        compiler_params=pltpu.CompilerParams(collective_id=0, has_side_effects=True),
    )(*operands)
    return out.reshape(rows, amino, width)


def solution(mesh):
    split = ("rep", "branch", "dap")
    placed = (
        P(split, None, None), P(split), P("rep"), P(split, None), P(split, None, None),
        P(), P(), P(), P(), P(), P(), P(), P(), P(), P(),
    )
    return jax.shard_map(
        functools.partial(on_device, mesh.shape["branch"], mesh.shape["dap"]),
        mesh=mesh,
        in_specs=placed,
        out_specs=P(split, None, None),
        check_vma=False,
    )
```

profile of v0, /device:TPU:0, one launch (start us, length us, event | category | flops | bytes accessed | tf_op | source)
XLA Modules:
  0.0 17.7 jit_solution(2384967582824454417)
XLA Ops:
  0.0 17.1 %shard_map.145 = bf16[128,128]{1,0:T(8,128)(2,1)S(1)} custom-call(bf16[512,256]{1,0:T(8,128)(2,1)} %bitcast.11, s32[1,16]{1,0:T(1,128)} %bitcast.16, s32[1,32]{1,0:T(1,128)} %bitcast.17, s32[4,32]{1,0:T(4,128)} %refs_3_.1, bf16[128,128]{1,0:T(8,128)(2,1)} %bitcast.12, f32[1,256]{1,0:T(1,128)} %bitcast.15, bf16[32,256]{1,0:T(8,128)(2,1)} %bitcast.13, ...), custom_call_target="tpu_custom_call" | custom-call | tf_op jit(solution)/shard_map/pallas_call | solution.py:320
  17.1 0.6 %copy.17 = bf16[4,32,128]{2,1,0:T(8,128)(2,1)} copy(bf16[4,32,128]{2,1,0:T(8,128)(2,1)S(1)} %bitcast.10) | data formatting | bytes 65536
where the time goes:
time: 17.9 us; the launch traced here: 17.7 us
  Pallas kernels  17.1 us (96%)
  local copies, waits for them, and re-layouts  0.62 us (3%)
    pallas_call x1, Pallas kernels, on_device(): pl.pallas_call(functools.partial(kernel, nb, nz), out_shape=pltpu.VMEM((r...  17.1 us
    unnamed x1, local copies, waits for them, and re-layouts  0.62 us

commit v1 on v0

--- a/solution.py
+++ b/solution.py
@@ -39,7 +39,7 @@
     (x_ref, hflag_ref, aflag_ref, class_ref, couple_ref, hgain_ref, wl_ref, wr_ref, wout_ref,
      embed_ref, cgain_ref, wedge_ref, wgate_ref, wfin_ref, tgain_ref) = held
     (
-    flag_all, right_all, left_send, left_all, tri_all, y_left, outer_buf, w_wide, w_perm, tri_buf,
+    flag_all, right_all, left_send, left_all, tri_all, y_left, outer_buf, w_wide, w_perm, tri_buf, mix_buf,
     flag_ssem, flag_rsem, right_ssem, right_rsem, right_fsem, left_ssem, left_rsem,
     tri_ssem, tri_rsem, tri_fsem,
     ) = scratch
@@ -59,7 +59,10 @@
     padded = -(-live // SUB) * SUB
     first = me * rows
 
-    same = [(branch, lax.rem(dap + step, nz)) for step in range(1, nz)]
+    low = 2 * dap < nz
+    same = [
+        (branch, jnp.where(low, k + (k >= dap), nz - 1 - k - (nz - 1 - k <= dap))) for k in range(nz - 1)
+    ]
     here = [(lax.rem(branch + step, nb), dap) for step in range(1, nb)]
     far = [(b[0], z[1]) for b in here for z in same]
     near = same + here
@@ -149,14 +152,20 @@
             recv_sem=rsem.at[slot], device_id=target(everyone[0]), device_id_type=MESH,
         ).wait_recv()
 
-    for peer in everyone:
-        d = index_of(peer)
-        push(flag_all.at[me], flag_all.at[me], flag_ssem.at[d], flag_rsem.at[me], peer)
-    for peer in near:
-        push(right_all.at[me], right_all.at[me], right_ssem.at[index_of(peer)], right_rsem.at[me], peer)
-    for peer in everyone:
+    def push_left(peer):
         d = index_of(peer)
         push(left_send.at[d], left_all.at[me], left_ssem.at[d], left_rsem.at[me], peer)
+        push(flag_all.at[me], flag_all.at[me], flag_ssem.at[d], flag_rsem.at[me], peer)
+
+    def push_right(peer):
+        push(right_all.at[me], right_all.at[me], right_ssem.at[index_of(peer)], right_rsem.at[me], peer)
+
+    push_right(here[0])
+    push_left(here[0])
+    for peer, other in reversed(list(zip(same, far))):
+        push_right(peer)
+        push_left(peer)
+        push_left(other)
     left_all[me] = left_send[me]
 
     for k in (8, 3, 4, 9, 10, 11, 12, 13, 14):
@@ -184,16 +193,24 @@
     key_pair = jnp.where(ilane > 0.5, key_pair, 0.0).astype(jnp.int32)
     pair_row = iota((1, pairs), 1) // amino
     sel_rows = live * rows
+    slots = rows * padded
+    slot = iota((slots, 1), 0)
+    gather = jnp.where(
+        (key_pair == lax.rem(slot, padded) + 1) & (pair_row == slot // padded), 1.0, 0.0
+    ).astype(BF16)
+    base_c = dot(gather, couple_ref[...]) + dot(dot(gather, onehot).astype(BF16), embed_ref[...])
     sel_m = iota((sel_rows, 1), 0)
-    sel_key = key_pair == sel_m // rows + 1
-    select_right = jnp.where(sel_key & (pair_row == lax.rem(sel_m, rows)), 1.0, 0.0).astype(BF16)
+    lane_slot = iota((1, slots), 1)
     select_left = jnp.concatenate(
-        [jnp.where(sel_key & (pair_row == i), 1.0, 0.0) for i in range(rows)], axis=0
+        [
+            jnp.where(lane_slot == sel_m // rows + i * padded, 1.0, 0.0)
+            for i in range(rows)
+        ],
+        axis=0,
     ).astype(BF16)
     wide_key = jnp.broadcast_to(lane_keys(amino), (amino, amino))
     key_col = jnp.sum(jnp.where(eye, wide_key, 0.0), axis=1, keepdims=True).astype(jnp.int32)
     key_col = jnp.concatenate([key_col] * rows, axis=0)
-    slots = rows * padded
     col = iota((pairs, slots), 1)
     expand = jnp.where(
         (key_col == lax.rem(col, padded) + 1) & (iota((pairs, slots), 0) // amino == col // padded),
@@ -242,20 +259,23 @@
             parts[i].append(block[i])
     packed = jnp.concatenate([jnp.concatenate(p, axis=1) for p in parts], axis=0).astype(BF16)
     product = dot(packed, w_perm[...])
-    high = product.astype(BF16)
-    low = (product - high.astype(F32)).astype(BF16)
-    projected = dot(expand, jnp.concatenate([high, low], axis=0))
-    updated = base + projected / number
-    pair = standardize(updated, cgain_ref[...]).astype(BF16)
-    right_two = dot(pair, wedge_ref[:, 2 * width :])
-    tri_right = (jax.nn.sigmoid(right_two[:, :width]) * right_two[:, width:]).astype(BF16)
-    tri_all[me] = dot(select_right, tri_right).astype(BF16)
-    for peer in near:
+    product = product / number
+    pair_c = standardize(base_c + product, cgain_ref[...]).astype(BF16)
+    right_two = dot(pair_c, wedge_ref[:, 2 * width :])
+    tri_right = jax.nn.sigmoid(right_two[:, :width]) * right_two[:, width:]
+    for i in range(rows):
+        mix_buf[pl.ds(i, padded, stride=rows), :] = tri_right[i * padded : (i + 1) * padded]
+    tri_all[me] = mix_buf[:sel_rows, :].astype(BF16)
+    for peer in here + same[::-1]:
         push(tri_all.at[me], tri_all.at[me], tri_ssem.at[index_of(peer)], tri_rsem.at[me], peer)
 
-    left_two = dot(pair, wedge_ref[:, : 2 * width])
+    left_two = dot(pair_c, wedge_ref[:, : 2 * width])
     tri_left = (jax.nn.sigmoid(left_two[:, :width]) * left_two[:, width:]).astype(BF16)
     spread_left = dot(select_left, tri_left)
+    high = product.astype(BF16)
+    low_part = (product - high.astype(F32)).astype(BF16)
+    updated = base + dot(expand, jnp.concatenate([high, low_part], axis=0))
+    pair = standardize(updated, cgain_ref[...]).astype(BF16)
     gate = jax.nn.sigmoid(dot(pair, wgate_ref[...]))
 
     def passing(peer):
@@ -335,6 +355,7 @@
             pltpu.VMEM((inner * inner, width), F32),
             pltpu.VMEM((inner * inner, width), BF16),
             pltpu.VMEM((rows * amino, width), F32),
+            pltpu.VMEM((rows * padded, width), F32),
             dma((n,)), dma((n,)),
             dma((n,)), dma((n,)), dma((nb, nz)),
             dma((n,)), dma((n,)),

time: 17.9 us -> 17.2 us (0.961)
  Pallas kernels: 17.1 us -> 16.4 us
    pallas_call x1, Pallas kernels: 17.1 us -> 16.4 us  [on_device(): pl.pallas_call(functools.partial(kernel, nb, nz), out_shape=pltpu.VMEM((r...]
where the time goes in v1:
time: 17.2 us; the launch traced here: 17 us
  Pallas kernels  16.4 us (95%)
  local copies, waits for them, and re-layouts  0.62 us (4%)
    pallas_call x1, Pallas kernels, on_device(): pl.pallas_call(functools.partial(kernel, nb, nz), out_shape=pltpu.VMEM((r...  16.4 us
    unnamed x1, local copies, waits for them, and re-layouts  0.62 us

profile of v1, /device:TPU:0, one launch (start us, length us, event | category | flops | bytes accessed | tf_op | source)
XLA Modules:
  0.0 17.0 jit_solution(2915829379947987773)
XLA Ops:
  0.0 16.4 %shard_map.145 = bf16[128,128]{1,0:T(8,128)(2,1)S(1)} custom-call(bf16[512,256]{1,0:T(8,128)(2,1)} %bitcast.11, s32[1,16]{1,0:T(1,128)} %bitcast.16, s32[1,32]{1,0:T(1,128)} %bitcast.17, s32[4,32]{1,0:T(4,128)} %refs_3_.1, bf16[128,128]{1,0:T(8,128)(2,1)} %bitcast.12, f32[1,256]{1,0:T(1,128)} %bitcast.15, bf16[32,256]{1,0:T(8,128)(2,1)} %bitcast.13, ...), custom_call_target="tpu_custom_call" | custom-call | tf_op jit(solution)/shard_map/pallas_call | solution.py:340
  16.4 0.6 %copy.17 = bf16[4,32,128]{2,1,0:T(8,128)(2,1)} copy(bf16[4,32,128]{2,1,0:T(8,128)(2,1)S(1)} %bitcast.10) | data formatting | bytes 65536

commit v2 on v0

v2 whole, which is shorter than its diff:
```python
import functools

import jax
import jax.numpy as jnp
from jax import lax
from jax.experimental import pallas as pl
from jax.experimental.pallas import tpu as pltpu
from jax.sharding import PartitionSpec as P

F32 = jnp.float32
BF16 = jnp.bfloat16
MESH = pl.DeviceIdType.MESH
OPERANDS = 15
LANES = 128
SUB = 8


def iota(shape, axis):
    return lax.broadcasted_iota(jnp.int32, shape, axis)


def dot(a, b):
    return jnp.dot(a, b, preferred_element_type=F32)


def standardize(values, gain):
    mean = jnp.mean(values, axis=-1, keepdims=True)
    centred = values - mean
    spread = jnp.mean(centred * centred, axis=-1, keepdims=True)
    return centred * lax.rsqrt(spread + 1e-05) * gain


def kernel(
    nb, nz,
    *refs,
):
    operands, out_ref, held = refs[:OPERANDS], refs[OPERANDS], refs[OPERANDS + 1 : 2 * OPERANDS + 1]
    in_sem, *scratch = refs[2 * OPERANDS + 1 :]
    (x_ref, hflag_ref, aflag_ref, class_all, couple_all, hgain_ref, wl_ref, wr_ref, wout_ref,
     embed_ref, cgain_ref, wedge_ref, wgate_ref, wfin_ref, tgain_ref) = held
    (
    flag_all, right_send, right_main, right_tail, left_send, left_all, left_last, tri_all, y_left, outer_buf,
    base_buf, base_send, base_last, product_all, edge_buf, spread_buf, own_buf, part_send, part_in, tri_buf,
    flag_sems, right_sems, tail_sems, left_sems, last_sems, base_sems, tri_ssem, tri_rsem, part_ssem, part_rsem,
    pair_ssem, pair_rsem, ready,
    ) = scratch
    n = nb * nz
    branch = lax.axis_index("branch")
    dap = lax.axis_index("dap")
    me = branch * nz + dap
    amino = aflag_ref.shape[1]
    seqs = hflag_ref.shape[1]
    rows = class_all.shape[1]
    inner = wl_ref.shape[0]
    width = couple_all.shape[2]
    reps = LANES // inner
    live = amino - 3 * amino // 8
    tiles = live // reps
    groups = -(-tiles // nb)
    even = tiles % nb == 0
    part = groups * reps
    main = (groups - 1) * LANES
    block_rows = nb * rows
    slots = part * block_rows
    firm = slots - reps * block_rows
    pairs = rows * amino
    chips = [k + (k >= dap) for k in range(nz - 1)]
    redo = nz > 2
    end = nz - 1
    order = []
    for k in range(nz - 1):
        rank = jnp.where(dap == 0, nz - 2, jnp.where(dap == end, end, dap - 1))
        rank = k + (k >= rank)
        order.append(jnp.where(rank < nz - 2, rank + 1, jnp.where(rank == nz - 2, 0, end)))
    other = nb - 1 - branch
    partner = (other, dap)
    everyone = [partner] + [(b, z) for z in chips for b in (branch, other)]

    def index_of(peer):
        return peer[0] * nz + peer[1]

    def target(peer):
        return {"branch": peer[0], "dap": peer[1]}

    barrier = pltpu.get_barrier_semaphore()
    pl.semaphore_signal(barrier, inc=1, device_id=target(partner), device_id_type=MESH)
    for b, z in everyone[1:]:

        @pl.when(z > dap)
        def _():
            pl.semaphore_signal(barrier, inc=1, device_id=target((b, z)), device_id_type=MESH)

    loads = {}
    for k in (2, 1, 0, 5, 6, 7, 8, 3, 4, 9, 10, 11, 12, 13, 14):
        place = held[k].at[branch] if k in (3, 4) else held[k]
        loads[k] = pltpu.make_async_copy(operands[k], place, in_sem.at[k])
        loads[k].start()

    pl.semaphore_wait(barrier, dap * nb + 1)
    for b, z in everyone[1:]:

        @pl.when(z < dap)
        def _():
            pl.semaphore_signal(ready.at[dap], inc=1, device_id=target((b, z)), device_id_type=MESH)

    if not even:

        @pl.when(branch > 0)
        def _():
            right_tail[...] = jnp.zeros(right_tail.shape, BF16)
            tri_all[:, firm:, :] = jnp.zeros((nz, slots - firm, width), BF16)

    loads[2].wait()
    loads[1].wait()
    aflag = jnp.broadcast_to(aflag_ref[...].astype(F32), (SUB, amino)).astype(BF16)
    hflag32 = hflag_ref[...].astype(F32)
    hflag = jnp.broadcast_to(hflag32, (SUB, seqs)).astype(BF16)

    def lane_keys(lanes):
        r = iota((amino, lanes), 0)
        k = lax.rem(iota((amino, lanes), 1), amino)
        count = dot(aflag, (r <= k).astype(BF16))
        alive = dot(aflag, (r == k).astype(BF16))
        return (count * alive)[0:1, :]

    flag_all[me] = jnp.broadcast_to(jnp.sum(hflag32, axis=1, keepdims=True), (1, LANES))

    total = seqs * amino
    key_x = lane_keys(total)
    hlane = dot(hflag, (iota((seqs, total), 0) == iota((seqs, total), 1) // amino).astype(BF16))[0:1, :]
    key_x = jnp.where(hlane > 0.5, key_x, 0.0).astype(jnp.int32)
    m_row = iota((live * seqs, 1), 0)
    same_seq = lax.rem(m_row, seqs) == iota((1, total), 1) // amino
    gather_right = jnp.where((key_x == m_row // seqs + 1) & same_seq, 1.0, 0.0).astype(BF16)
    lane_group = iota((1, LANES), 1) // inner
    alane = dot(
        aflag,
        (iota((amino, amino * inner), 0) == iota((amino, amino * inner), 1) // inner).astype(BF16),
    )[0:1, :]

    for k in (0, 5, 6, 7):
        loads[k].wait()
    normed = standardize(x_ref[...].astype(F32), hgain_ref[...]).astype(BF16)
    w_both = jnp.concatenate([wl_ref[...]] * reps + [wr_ref[...]] * reps, axis=0)
    sides = lax.dot_general(
        normed, w_both, (((1,), (1,)), ((), ())), preferred_element_type=F32
    )
    y_left[...] = sides[:, :LANES]
    right_rows = dot(gather_right, sides[:, LANES:].astype(BF16))
    for b in range(nb):
        for t in range(min(groups, tiles - b * groups)):
            begin = (b * part + t * reps) * seqs
            block = right_rows[begin : begin + seqs]
            for g in range(1, reps):
                block = jnp.where(
                    lane_group == g, right_rows[begin + g * seqs : begin + (g + 1) * seqs], block
                )
            right_send[b, t] = block.astype(BF16)
    for d in range(n):
        block = y_left[pl.ds(d * rows, seqs, stride=amino), :]
        for g in range(1, rows):
            block = jnp.where(
                lane_group == g, y_left[pl.ds(d * rows + g, seqs, stride=amino), :], block
            )
        left_send[d % nz, d // nz] = (block * alane[:, d * LANES : (d + 1) * LANES]).astype(BF16)


    def push(src, dst, ssem, rsem, peer, when=None):
        copy = pltpu.make_async_remote_copy(
            src_ref=src, dst_ref=dst, send_sem=ssem, recv_sem=rsem,
            device_id=target(peer), device_id_type=MESH,
        )
        guarded(when, copy.start)

    def tail(b):
        return None if even else b == 0

    def guarded(when, act):
        if when is None:
            act()
        else:
            pl.when(when)(act)

    def drain(ref, ssem, when=None):
        wait = pltpu.make_async_remote_copy(
            src_ref=ref, dst_ref=ref, send_sem=ssem, recv_sem=ssem,
            device_id=target(partner), device_id_type=MESH,
        ).wait_send
        guarded(when, wait)

    def arrived(ref, rsem, when=None):
        wait = pltpu.make_async_remote_copy(
            src_ref=ref, dst_ref=ref, send_sem=rsem,
            recv_sem=rsem, device_id=target(partner), device_id_type=MESH,
        ).wait_recv
        guarded(when, wait)

    def share(ref, k):
        push(ref.at[branch], ref.at[branch], pair_ssem.at[k], pair_rsem.at[k], partner)

    for k in (3, 4):
        loads[k].wait()
    def push_block(peer):
        b, z = peer
        push(left_send.at[z], left_all.at[me], left_sems.at[0], left_sems.at[1], peer)
        push(right_send.at[b, : groups - 1], right_main.at[me], right_sems.at[0], right_sems.at[1], peer)
        push(right_send.at[b, groups - 1], right_tail.at[me], tail_sems.at[0], tail_sems.at[1], peer, tail(b))
        push(flag_all.at[me], flag_all.at[me], flag_sems.at[0], flag_sems.at[1], peer)

    push_block(partner)
    share(class_all, 0)
    share(couple_all, 1)
    for z in order:

        @pl.when(z > dap)
        def _():
            pl.semaphore_wait(ready.at[z], nb)

        push_block((branch, z))
        push_block((other, z))
    if redo:
        push(left_send.at[end], left_last.at[me], last_sems.at[0], last_sems.at[1], (other, 0))
        push(left_send.at[end], left_last.at[me], last_sems.at[0], last_sems.at[1], (branch, 0), dap != 0)

        @pl.when(dap == 0)
        def _():
            left_last[me] = left_send[end]

    right_main[me] = right_send[branch, : groups - 1]
    if even:
        right_tail[me] = right_send[branch, groups - 1]
    else:

        @pl.when(branch == 0)
        def _():
            right_tail[me] = right_send[0, groups - 1]

    left_all[me] = left_send[dap]

    for k in (8, 9, 10, 11, 12, 13, 14):
        loads[k].wait()
    chip_pairs = nb * pairs
    lane_pair = iota((1, chip_pairs), 1)
    key_pair = lane_keys(chip_pairs)
    residue = (lane_pair // pairs * nz + dap) * rows + lax.rem(lane_pair // amino, rows)
    ilane = dot(aflag, (iota((amino, chip_pairs), 0) == residue).astype(BF16))[0:1, :]
    key_pair = jnp.where(ilane > 0.5, key_pair, 0.0).astype(jnp.int32)
    slot = iota((slots, 1), 0)
    gather = jnp.where(
        (key_pair == branch * part + slot // block_rows + 1) & (lane_pair // amino == lax.rem(slot, block_rows)),
        1.0,
        0.0,
    ).astype(BF16)
    eye = iota((amino, amino), 0) == iota((amino, amino), 1)
    wide_key = jnp.broadcast_to(lane_keys(amino), (amino, amino))
    key_col = jnp.sum(jnp.where(eye, wide_key, 0.0), axis=1, keepdims=True).astype(jnp.int32)
    key_col = jnp.concatenate([key_col] * rows, axis=0)
    col = iota((1, nb * slots), 1)
    expand = jnp.where(
        (key_col == col // block_rows + 1)
        & (iota((pairs, 1), 0) // amino + branch * rows == lax.rem(col, block_rows)),
        1.0,
        0.0,
    ).astype(BF16)
    expand = jnp.concatenate([expand, expand], axis=1)
    arrived(class_all.at[other], pair_rsem.at[0])
    arrived(couple_all.at[other], pair_rsem.at[1])
    bins = embed_ref.shape[0]
    hot = []
    for b in range(nb):
        for i in range(rows):
            column = jnp.sum(
                jnp.where(eye, class_all[b, i : i + 1, :], 0).astype(F32), axis=1, keepdims=True
            ).astype(jnp.int32)
            hot.append(jnp.where(column == iota((amino, bins), 1), 1.0, 0.0))
    onehot = jnp.concatenate(hot, axis=0).astype(BF16)
    couple = couple_all[...].reshape(chip_pairs, width)
    base_buf[...] = (couple.astype(F32) + dot(onehot, embed_ref[...])).reshape(nb, pairs, width)
    base_c = dot(gather, couple) + dot(dot(gather, onehot).astype(BF16), embed_ref[...])

    if redo:

        @pl.when(dap == end)
        def _():
            base_send[...] = base_c.astype(BF16)

        push(base_send, base_last, base_sems.at[0], base_sems.at[1], (branch, 0), dap == end)

    arrived(right_main.at[: n - 1], right_sems.at[1])
    arrived(right_tail.at[: n - 1], tail_sems.at[1], tail(branch))
    arrived(left_all.at[: n - 1], left_sems.at[1])
    arrived(flag_all.at[: n - 1], flag_sems.at[1])

    number = jnp.maximum(jnp.sum(flag_all[...], axis=0), 1.0)
    right = jnp.concatenate(
        [right_main[:, t].reshape(n * seqs, LANES) for t in range(groups - 1)]
        + [right_tail[...].reshape(n * seqs, LANES)],
        axis=1,
    )
    lane = iota((1, LANES), 1)

    def middle(left_ref, base):
        left = jnp.concatenate([left_ref[:, b].reshape(n * seqs, LANES) for b in range(nb)], axis=1)
        outer = lax.dot_general(left, right, (((0,), (0,)), ((), ())), preferred_element_type=F32)
        for t in range(groups):
            outer_buf[t] = outer[:, t * LANES : (t + 1) * LANES]
        parts = [[] for _ in range(part)]
        for t in range(groups):
            for q in range(inner // reps):
                block = [outer_buf[t, pl.ds(q * reps + g, block_rows, stride=inner), :] for g in range(reps)]
                span = reps // 2
                while span:
                    upper = (lane // (span * inner)) % 2 == 1
                    new = list(block)
                    for a in range(reps):
                        if a & span:
                            continue
                        b = a | span
                        shift = span * inner
                        new[a] = jnp.where(upper, pltpu.roll(block[b], shift, 1), block[a])
                        new[b] = jnp.where(upper, block[b], pltpu.roll(block[a], LANES - shift, 1))
                    block = new
                    span //= 2
                for g in range(reps):
                    parts[t * reps + g].append(block[g])
        packed = jnp.concatenate([jnp.concatenate(p, axis=1) for p in parts], axis=0).astype(BF16)
        product = dot(packed, wout_ref[...]) / number
        pair_c = standardize(base + product, cgain_ref[...]).astype(BF16)
        right_two = dot(pair_c, wedge_ref[:, 2 * width :])
        tri_right = jax.nn.sigmoid(right_two[:, :width]) * right_two[:, width:]
        return product, pair_c, tri_right.astype(BF16)

    product, pair_c, tri_all[dap] = middle(left_all, base_c)
    full = tail(branch)
    short = None if even else branch != 0

    def tri_block(z, size):
        return tri_all.at[z, :size]

    for z in chips:
        skip = redo & (dap == end) & (z == 0)
        if even:
            push(tri_all.at[dap], tri_all.at[dap], tri_ssem.at[0], tri_rsem.at[dap], (branch, z), ~skip)
        else:
            for size, when in ((slots, full), (firm, short)):
                push(
                    tri_block(dap, size), tri_block(dap, size), tri_ssem.at[0], tri_rsem.at[dap], (branch, z),
                    when & ~skip,
                )

    product_all[branch] = product
    share(product_all, 2)
    left_two = dot(pair_c, wedge_ref[:, : 2 * width])
    edge_buf[...] = (jax.nn.sigmoid(left_two[:, :width]) * left_two[:, width:]).astype(BF16).astype(F32)
    for i in range(block_rows):
        for k in range(part):
            row = edge_buf[k * block_rows + i : k * block_rows + i + 1, :]
            spread_buf[i, k * SUB : (k + 1) * SUB, :] = jnp.broadcast_to(row, (SUB, width))

    def triangle(z, side, store):
        block = tri_all[z].astype(F32)
        for i in range(rows):
            both = spread_buf[side * rows + i] * block
            store[z, i] = jnp.sum(both.reshape(part, SUB, width), axis=0)

    def contribute(z):
        triangle(z, other, part_send)
        push(part_send.at[z], part_in.at[z], part_ssem.at[0], part_rsem.at[z], partner)
        triangle(z, branch, own_buf)

    def settle(z):
        arrived(part_in.at[z], part_rsem.at[z])
        for i in range(rows):
            total = own_buf[z, i] + part_in[z, i]
            for b in range(nb):
                row = i * amino + (b * nz + z) * rows
                tri_buf[pl.ds(pl.multiple_of(row, rows), rows), :] = total[b * rows : (b + 1) * rows]

    contribute(dap)
    if redo:

        @pl.when(dap == 0)
        def _():
            arrived(left_last.at[: n - 1], last_sems.at[1])
            arrived(base_last, base_sems.at[1])
            tri_all[end] = middle(left_last, base_last[...].astype(F32))[2]
            contribute(end)

    late = [jnp.where(dap == 0, k + 1, (k + 1 + (k + 1 >= dap)) % nz) for k in range(nz - 1)]
    late = [jnp.where((dap == 0) | (k < nz - 2), z, 0) for k, z in enumerate(late)]
    for k, z in enumerate(late):
        skip = redo & (dap == 0) & (z == end)

        @pl.when(~skip)
        def _():
            if even:
                arrived(tri_all.at[z], tri_rsem.at[z])
            else:
                arrived(tri_block(z, slots), tri_rsem.at[z], full)
                arrived(tri_block(z, firm), tri_rsem.at[z], short)
            contribute(z)
    arrived(product_all.at[other], pair_rsem.at[2])
    whole = product_all[...].reshape(nb * slots, width)
    high = whole.astype(BF16)
    rest = (whole - high.astype(F32)).astype(BF16)
    updated = base_buf[branch] + dot(expand, jnp.concatenate([high, rest], axis=0))
    pair = standardize(updated, cgain_ref[...]).astype(BF16)
    gate = jax.nn.sigmoid(dot(pair, wgate_ref[...]))
    for z in [dap] + late:
        settle(z)
    tri = standardize(tri_buf[...], tgain_ref[...]).astype(BF16)
    out_ref[...] = (updated + gate * dot(tri, wfin_ref[...])).astype(BF16)
    drain(left_all.at[: n - 1], left_sems.at[0])
    drain(right_main.at[: n - 1], right_sems.at[0])
    if even:
        drain(right_tail.at[: n - 1], tail_sems.at[0])
    else:
        drain(right_tail.at[: nz - 1], tail_sems.at[0], full)
        drain(right_tail.at[:nz], tail_sems.at[0], short)
    drain(flag_all.at[: n - 1], flag_sems.at[0])
    if redo:
        drain(left_last.at[:1], last_sems.at[0], dap == 0)
        drain(left_last.at[:nb], last_sems.at[0], dap != 0)
        drain(base_send, base_sems.at[0], dap == end)
    for fewer, last in ((1, redo & (dap == end)), (0, ~(redo & (dap == end)))):
        if even:
            drain(tri_all.at[: nz - 1 - fewer], tri_ssem.at[0], last)
        else:
            drain(tri_all.at[: nz - 1 - fewer], tri_ssem.at[0], last & full)
            drain(tri_all.at[: nz - 1 - fewer, :firm], tri_ssem.at[0], last & short)
    drain(part_send, part_ssem.at[0])
    for k, ref in enumerate((class_all, couple_all, product_all)):
        drain(ref.at[branch], pair_ssem.at[k])


def on_device(nb, nz, x, hflags, aflags, classes, couple, hgain, wl, wr, wout, embed, cgain, wedge, wgate, wfin, tgain):
    n = nb * nz
    seqs, amino, depth = x.shape
    rows, _, width = couple.shape
    inner = wl.shape[1]
    live = amino - 3 * amino // 8
    groups = -(-(live // (LANES // inner)) // nb)
    part = groups * (LANES // inner)
    slots = part * nb * rows
    dma = pltpu.SemaphoreType.DMA
    operands = (
        x.reshape(seqs * amino, depth), hflags.reshape(1, seqs), aflags.reshape(1, amino), classes,
        couple.reshape(rows * amino, width), hgain.reshape(1, depth), wl.T, wr.T, wout, embed,
        cgain.reshape(1, width), wedge, wgate, wfin, tgain.reshape(1, width),
    )
    held = [pltpu.VMEM((nb, *a.shape) if k in (3, 4) else a.shape, a.dtype) for k, a in enumerate(operands)]
    out = pl.pallas_call(
        functools.partial(kernel, nb, nz),
        out_shape=pltpu.VMEM((rows * amino, width), BF16),
        in_specs=[pl.BlockSpec(memory_space=pl.ANY)] * OPERANDS,
        out_specs=pl.BlockSpec(memory_space=pltpu.VMEM),
        scratch_shapes=held
        + [
            dma((OPERANDS,)),
            pltpu.VMEM((n, 1, LANES), F32),
            pltpu.VMEM((nb, groups, seqs, LANES), BF16),
            pltpu.VMEM((n, groups - 1, seqs, LANES), BF16),
            pltpu.VMEM((n, seqs, LANES), BF16),
            pltpu.VMEM((nz, nb, seqs, LANES), BF16),
            pltpu.VMEM((n, nb, seqs, LANES), BF16),
            pltpu.VMEM((n, nb, seqs, LANES), BF16),
            pltpu.VMEM((nz, slots, width), BF16),
            pltpu.VMEM((seqs * amino, LANES), F32),
            pltpu.VMEM((groups, nb * LANES, LANES), F32),
            pltpu.VMEM((nb, rows * amino, width), F32),
            pltpu.VMEM((slots, width), BF16),
            pltpu.VMEM((slots, width), BF16),
            pltpu.VMEM((nb, slots, width), F32),
            pltpu.VMEM((slots, width), F32),
            pltpu.VMEM((nb * rows, slots, width), F32),
            pltpu.VMEM((nz, rows, SUB, width), F32),
            pltpu.VMEM((nz, rows, SUB, width), F32),
            pltpu.VMEM((nz, rows, SUB, width), F32),
            pltpu.VMEM((rows * amino, width), F32),
        ]
        + [dma((2,))] * 6
        + [dma((1,)), dma((nz,)), dma((1,)), dma((nz,)), dma((3,)), dma((3,))]
        + [pltpu.SemaphoreType.REGULAR((nz,))],
        compiler_params=pltpu.CompilerParams(collective_id=0, has_side_effects=True),
    )(*operands)
    return out.reshape(rows, amino, width)


def solution(mesh):
    split = ("rep", "branch", "dap")
    placed = (
        P(split, None, None), P(split), P("rep"), P(split, None), P(split, None, None),
        P(), P(), P(), P(), P(), P(), P(), P(), P(), P(),
    )
    return jax.shard_map(
        functools.partial(on_device, mesh.shape["branch"], mesh.shape["dap"]),
        mesh=mesh,
        in_specs=placed,
        out_specs=P(split, None, None),
        check_vma=False,
    )
```

time: 17.9 us -> 15.4 us (0.86)
  the two profiles are of different devices: /device:TPU:0 before, /device:TPU:1 now
where the time goes in v2:
time: 15.4 us; the launch traced here: 15.3 us
  Pallas kernels  14.6 us (95%)
  local copies, waits for them, and re-layouts  0.62 us (4%)
    pallas_call x1, Pallas kernels, on_device(): pl.pallas_call(functools.partial(kernel, nb, nz), out_shape=pltpu.VMEM((r...  14.6 us
    unnamed x1, local copies, waits for them, and re-layouts  0.62 us

profile of v2, /device:TPU:1, one launch (start us, length us, event | category | flops | bytes accessed | tf_op | source)
XLA Modules:
  0.0 15.3 jit_solution(14628854484100338086)
XLA Ops:
  0.0 14.6 %shard_map.145 = bf16[128,128]{1,0:T(8,128)(2,1)S(1)} custom-call(bf16[512,256]{1,0:T(8,128)(2,1)} %bitcast.11, s32[1,16]{1,0:T(1,128)} %bitcast.16, s32[1,32]{1,0:T(1,128)} %bitcast.17, s32[4,32]{1,0:T(4,128)} %refs_3_.1, bf16[128,128]{1,0:T(8,128)(2,1)} %bitcast.12, f32[1,256]{1,0:T(1,128)} %bitcast.15, bf16[32,256]{1,0:T(8,128)(2,1)} %bitcast.13, ...), custom_call_target="tpu_custom_call" | custom-call | tf_op jit(solution)/shard_map/pallas_call | solution.py:452
  14.7 0.6 %copy.17 = bf16[4,32,128]{2,1,0:T(8,128)(2,1)} copy(bf16[4,32,128]{2,1,0:T(8,128)(2,1)S(1)} %bitcast.10) | data formatting | bytes 65536

commit v3 on v2

--- a/solution.py
+++ b/solution.py
@@ -39,9 +39,9 @@
     (x_ref, hflag_ref, aflag_ref, class_all, couple_all, hgain_ref, wl_ref, wr_ref, wout_ref,
      embed_ref, cgain_ref, wedge_ref, wgate_ref, wfin_ref, tgain_ref) = held
     (
-    flag_all, right_send, right_main, right_tail, left_send, left_all, left_last, tri_all, y_left, outer_buf,
-    base_buf, base_send, base_last, product_all, edge_buf, spread_buf, own_buf, part_send, part_in, tri_buf,
-    flag_sems, right_sems, tail_sems, left_sems, last_sems, base_sems, tri_ssem, tri_rsem, part_ssem, part_rsem,
+    flag_all, right_send, right_all, left_send, left_all, left_last, tri_all, y_left, outer_buf,
+    base_buf, base_send, base_last, product_all, edge_buf, spread_buf, own_buf, part_send, part_in, tri_buf, updated_buf, gate_buf,
+    flag_sems, right_sems, pass_sems, last_sems, base_sems, left_rsem, tri_ssem, tri_rsem, part_ssem, part_rsem,
     pair_ssem, pair_rsem, ready,
     ) = scratch
     n = nb * nz
@@ -59,11 +59,14 @@
     groups = -(-tiles // nb)
     even = tiles % nb == 0
     part = groups * reps
-    main = (groups - 1) * LANES
+    most = groups
+    least = most if even else most - 1
     block_rows = nb * rows
     slots = part * block_rows
     firm = slots - reps * block_rows
     pairs = rows * amino
+    side = nb - 1 - branch
+    wide = nb - 1
     chips = [k + (k >= dap) for k in range(nz - 1)]
     redo = nz > 2
     end = nz - 1
@@ -91,23 +94,29 @@
             pl.semaphore_signal(barrier, inc=1, device_id=target((b, z)), device_id_type=MESH)
 
     loads = {}
-    for k in (2, 1, 0, 5, 6, 7, 8, 3, 4, 9, 10, 11, 12, 13, 14):
+    for k in (2,1,0,5,6,7,8,3,4,9,10,11,12,13,14):
         place = held[k].at[branch] if k in (3, 4) else held[k]
         loads[k] = pltpu.make_async_copy(operands[k], place, in_sem.at[k])
-        loads[k].start()
+        if k == 0:
+            step = x_ref.shape[0] // 8
+            for j in range(8):
+                piece = pl.ds(j * step, step)
+                pltpu.make_async_copy(operands[0].at[piece], x_ref.at[piece], in_sem.at[0]).start()
+        else:
+            loads[k].start()
 
     pl.semaphore_wait(barrier, dap * nb + 1)
     for b, z in everyone[1:]:
 
         @pl.when(z < dap)
         def _():
-            pl.semaphore_signal(ready.at[dap], inc=1, device_id=target((b, z)), device_id_type=MESH)
+            pl.semaphore_signal(ready.at[dap - 1], inc=1, device_id=target((b, z)), device_id_type=MESH)
 
     if not even:
 
-        @pl.when(branch > 0)
-        def _():
-            right_tail[...] = jnp.zeros(right_tail.shape, BF16)
+        @pl.when(branch != wide)
+        def _():
+            right_all[:, least:] = jnp.zeros((n, most - least, seqs, LANES), BF16)
             tri_all[:, firm:, :] = jnp.zeros((nz, slots - firm, width), BF16)
 
     loads[2].wait()
@@ -126,12 +135,14 @@
     flag_all[me] = jnp.broadcast_to(jnp.sum(hflag32, axis=1, keepdims=True), (1, LANES))
 
     total = seqs * amino
-    key_x = lane_keys(total)
+    span = SUB * amino
+    key_x = lane_keys(span)
     hlane = dot(hflag, (iota((seqs, total), 0) == iota((seqs, total), 1) // amino).astype(BF16))[0:1, :]
-    key_x = jnp.where(hlane > 0.5, key_x, 0.0).astype(jnp.int32)
-    m_row = iota((live * seqs, 1), 0)
-    same_seq = lax.rem(m_row, seqs) == iota((1, total), 1) // amino
-    gather_right = jnp.where((key_x == m_row // seqs + 1) & same_seq, 1.0, 0.0).astype(BF16)
+    gather_right = []
+    for h in range(seqs // SUB):
+        code = (key_x - 1.0) * SUB + (iota((1, span), 1) // amino).astype(F32)
+        code = jnp.where(hlane[:, h * span : (h + 1) * span] * key_x > 0.5, code, -1.0).astype(jnp.int32)
+        gather_right.append(jnp.where(iota((live * SUB, 1), 0) == code, 1.0, 0.0).astype(BF16))
     lane_group = iota((1, LANES), 1) // inner
     alane = dot(
         aflag,
@@ -145,22 +156,27 @@
     sides = lax.dot_general(
         normed, w_both, (((1,), (1,)), ((), ())), preferred_element_type=F32
     )
-    y_left[...] = sides[:, :LANES]
-    right_rows = dot(gather_right, sides[:, LANES:].astype(BF16))
+    for i in range(seqs):
+        y_left[pl.ds(i * (amino + 1), amino), :] = sides[i * amino : (i + 1) * amino, :LANES]
+    right_rows = [
+        dot(gather, sides[h * span : (h + 1) * span, LANES:].astype(BF16)) for h, gather in enumerate(gather_right)
+    ]
+
+    def right_of(k):
+        return jnp.concatenate([part_rows[k * SUB : (k + 1) * SUB] for part_rows in right_rows], axis=0)
+
     for b in range(nb):
-        for t in range(min(groups, tiles - b * groups)):
-            begin = (b * part + t * reps) * seqs
-            block = right_rows[begin : begin + seqs]
+        for t in range(min(groups, tiles - (nb - 1 - b) * groups)):
+            begin = (nb - 1 - b) * part + t * reps
+            block = right_of(begin)
             for g in range(1, reps):
-                block = jnp.where(
-                    lane_group == g, right_rows[begin + g * seqs : begin + (g + 1) * seqs], block
-                )
+                block = jnp.where(lane_group == g, right_of(begin + g), block)
             right_send[b, t] = block.astype(BF16)
     for d in range(n):
-        block = y_left[pl.ds(d * rows, seqs, stride=amino), :]
+        block = y_left[pl.ds(d * rows, seqs, stride=amino + 1), :]
         for g in range(1, rows):
             block = jnp.where(
-                lane_group == g, y_left[pl.ds(d * rows + g, seqs, stride=amino), :], block
+                lane_group == g, y_left[pl.ds(d * rows + g, seqs, stride=amino + 1), :], block
             )
         left_send[d % nz, d // nz] = (block * alane[:, d * LANES : (d + 1) * LANES]).astype(BF16)
 
@@ -172,9 +188,6 @@
         )
         guarded(when, copy.start)
 
-    def tail(b):
-        return None if even else b == 0
-
     def guarded(when, act):
         if when is None:
             act()
@@ -198,44 +211,49 @@
     def share(ref, k):
         push(ref.at[branch], ref.at[branch], pair_ssem.at[k], pair_rsem.at[k], partner)
 
+    def push_right(b, z, when=None):
+        size = most if even or b == wide else least
+        push(
+            right_send.at[b, :size], right_all.at[me, :size], right_sems.at[0], right_sems.at[1], (b, z), when
+        )
+
+    def push_left(z):
+        push(left_send.at[z], left_all.at[me], pass_sems.at[0], left_rsem.at[dap], (branch, z))
+
+    for z in order:
+
+        @pl.when(z > dap)
+        def _():
+            pl.semaphore_wait(ready.at[z - 1], nb)
+
+        push_left(z)
+        if redo:
+            push(left_send.at[end], left_last.at[me], last_sems.at[0], last_sems.at[1], (branch, 0), z == 0)
+        for b in range(nb):
+            push_right(b, z)
+        for b in range(nb):
+            push(flag_all.at[me], flag_all.at[me], flag_sems.at[0], flag_sems.at[1], (b, z))
+    for b in range(nb):
+        push_right(b, dap, branch != b)
+    push(left_send.at[dap], left_all.at[me], pass_sems.at[0], pass_sems.at[1], partner)
+    push(flag_all.at[me], flag_all.at[me], flag_sems.at[0], flag_sems.at[1], partner)
     for k in (3, 4):
         loads[k].wait()
-    def push_block(peer):
-        b, z = peer
-        push(left_send.at[z], left_all.at[me], left_sems.at[0], left_sems.at[1], peer)
-        push(right_send.at[b, : groups - 1], right_main.at[me], right_sems.at[0], right_sems.at[1], peer)
-        push(right_send.at[b, groups - 1], right_tail.at[me], tail_sems.at[0], tail_sems.at[1], peer, tail(b))
-        push(flag_all.at[me], flag_all.at[me], flag_sems.at[0], flag_sems.at[1], peer)
-
-    push_block(partner)
     share(class_all, 0)
     share(couple_all, 1)
-    for z in order:
-
-        @pl.when(z > dap)
-        def _():
-            pl.semaphore_wait(ready.at[z], nb)
-
-        push_block((branch, z))
-        push_block((other, z))
+    left_all[me] = left_send[dap]
+    right_all[me, :least] = right_send[branch, :least]
+    if not even:
+
+        @pl.when(branch == wide)
+        def _():
+            right_all[me, least:] = right_send[wide, least:]
+
     if redo:
-        push(left_send.at[end], left_last.at[me], last_sems.at[0], last_sems.at[1], (other, 0))
-        push(left_send.at[end], left_last.at[me], last_sems.at[0], last_sems.at[1], (branch, 0), dap != 0)
 
         @pl.when(dap == 0)
         def _():
             left_last[me] = left_send[end]
-
-    right_main[me] = right_send[branch, : groups - 1]
-    if even:
-        right_tail[me] = right_send[branch, groups - 1]
-    else:
-
-        @pl.when(branch == 0)
-        def _():
-            right_tail[me] = right_send[0, groups - 1]
-
-    left_all[me] = left_send[dap]
 
     for k in (8, 9, 10, 11, 12, 13, 14):
         loads[k].wait()
@@ -247,7 +265,7 @@
     key_pair = jnp.where(ilane > 0.5, key_pair, 0.0).astype(jnp.int32)
     slot = iota((slots, 1), 0)
     gather = jnp.where(
-        (key_pair == branch * part + slot // block_rows + 1) & (lane_pair // amino == lax.rem(slot, block_rows)),
+        (key_pair == side * part + slot // block_rows + 1) & (lane_pair // amino == lax.rem(slot, block_rows)),
         1.0,
         0.0,
     ).astype(BF16)
@@ -257,7 +275,7 @@
     key_col = jnp.concatenate([key_col] * rows, axis=0)
     col = iota((1, nb * slots), 1)
     expand = jnp.where(
-        (key_col == col // block_rows + 1)
+        (key_col == (nb - 1 - col // slots) * part + lax.rem(col, slots) // block_rows + 1)
         & (iota((pairs, 1), 0) // amino + branch * rows == lax.rem(col, block_rows)),
         1.0,
         0.0,
@@ -286,28 +304,38 @@
 
         push(base_send, base_last, base_sems.at[0], base_sems.at[1], (branch, 0), dap == end)
 
-    arrived(right_main.at[: n - 1], right_sems.at[1])
-    arrived(right_tail.at[: n - 1], tail_sems.at[1], tail(branch))
-    arrived(left_all.at[: n - 1], left_sems.at[1])
+    for z in chips:
+        d = branch * nz + z
+        arrived(left_all.at[d], left_rsem.at[z])
+        push(left_all.at[d], left_all.at[d], pass_sems.at[0], pass_sems.at[1], partner)
+    if redo:
+        arrived(left_last.at[: nz - 1], last_sems.at[1], dap == 0)
+        lasts = left_last.at[pl.ds(branch * nz, nz)]
+        push(lasts, lasts, last_sems.at[2], last_sems.at[3], partner, dap == 0)
+    if even:
+        arrived(right_all.at[: n - 1], right_sems.at[1])
+    else:
+        arrived(right_all.at[: n - 1], right_sems.at[1], branch == wide)
+        arrived(right_all.at[: n - 1, :least], right_sems.at[1], branch != wide)
+    arrived(left_all.at[:nz], pass_sems.at[1])
     arrived(flag_all.at[: n - 1], flag_sems.at[1])
 
     number = jnp.maximum(jnp.sum(flag_all[...], axis=0), 1.0)
-    right = jnp.concatenate(
-        [right_main[:, t].reshape(n * seqs, LANES) for t in range(groups - 1)]
-        + [right_tail[...].reshape(n * seqs, LANES)],
-        axis=1,
-    )
+    right = jnp.concatenate([right_all[:, t].reshape(n * seqs, LANES) for t in range(groups)], axis=1)
     lane = iota((1, LANES), 1)
 
     def middle(left_ref, base):
         left = jnp.concatenate([left_ref[:, b].reshape(n * seqs, LANES) for b in range(nb)], axis=1)
         outer = lax.dot_general(left, right, (((0,), (0,)), ((), ())), preferred_element_type=F32)
         for t in range(groups):
-            outer_buf[t] = outer[:, t * LANES : (t + 1) * LANES]
+            for i in range(block_rows):
+                outer_buf[t, pl.ds(i * (inner + 1), inner), :] = outer[
+                    i * inner : (i + 1) * inner, t * LANES : (t + 1) * LANES
+                ]
         parts = [[] for _ in range(part)]
         for t in range(groups):
             for q in range(inner // reps):
-                block = [outer_buf[t, pl.ds(q * reps + g, block_rows, stride=inner), :] for g in range(reps)]
+                block = [outer_buf[t, pl.ds(q * reps + g, block_rows, stride=inner + 1), :] for g in range(reps)]
                 span = reps // 2
                 while span:
                     upper = (lane // (span * inner)) % 2 == 1
@@ -331,8 +359,8 @@
         return product, pair_c, tri_right.astype(BF16)
 
     product, pair_c, tri_all[dap] = middle(left_all, base_c)
-    full = tail(branch)
-    short = None if even else branch != 0
+    full = None if even else branch == wide
+    short = None if even else branch != wide
 
     def tri_block(z, size):
         return tri_all.at[z, :size]
@@ -365,11 +393,10 @@
 
     def contribute(z):
         triangle(z, other, part_send)
-        push(part_send.at[z], part_in.at[z], part_ssem.at[0], part_rsem.at[z], partner)
+        push(part_send.at[z], part_in.at[z], part_ssem.at[0], part_rsem.at[0], partner)
         triangle(z, branch, own_buf)
 
     def settle(z):
-        arrived(part_in.at[z], part_rsem.at[z])
         for i in range(rows):
             total = own_buf[z, i] + part_in[z, i]
             for b in range(nb):
@@ -381,11 +408,22 @@
 
         @pl.when(dap == 0)
         def _():
-            arrived(left_last.at[: n - 1], last_sems.at[1])
+            arrived(left_last.at[:nz], last_sems.at[3])
             arrived(base_last, base_sems.at[1])
             tri_all[end] = middle(left_last, base_last[...].astype(F32))[2]
             contribute(end)
 
+    def refresh():
+        arrived(product_all.at[other], pair_rsem.at[2])
+        whole = product_all[...].reshape(nb * slots, width)
+        high = whole.astype(BF16)
+        rest = (whole - high.astype(F32)).astype(BF16)
+        updated = base_buf[branch] + dot(expand, jnp.concatenate([high, rest], axis=0))
+        pair = standardize(updated, cgain_ref[...]).astype(BF16)
+        updated_buf[...] = updated
+        gate_buf[...] = jax.nn.sigmoid(dot(pair, wgate_ref[...]))
+
+    pl.when(dap != 0)(refresh)
     late = [jnp.where(dap == 0, k + 1, (k + 1 + (k + 1 >= dap)) % nz) for k in range(nz - 1)]
     late = [jnp.where((dap == 0) | (k < nz - 2), z, 0) for k, z in enumerate(late)]
     for k, z in enumerate(late):
@@ -399,28 +437,21 @@
                 arrived(tri_block(z, slots), tri_rsem.at[z], full)
                 arrived(tri_block(z, firm), tri_rsem.at[z], short)
             contribute(z)
-    arrived(product_all.at[other], pair_rsem.at[2])
-    whole = product_all[...].reshape(nb * slots, width)
-    high = whole.astype(BF16)
-    rest = (whole - high.astype(F32)).astype(BF16)
-    updated = base_buf[branch] + dot(expand, jnp.concatenate([high, rest], axis=0))
-    pair = standardize(updated, cgain_ref[...]).astype(BF16)
-    gate = jax.nn.sigmoid(dot(pair, wgate_ref[...]))
-    for z in [dap] + late:
+    pl.when(dap == 0)(refresh)
+    arrived(part_in, part_rsem.at[0])
+    for z in range(nz):
         settle(z)
     tri = standardize(tri_buf[...], tgain_ref[...]).astype(BF16)
-    out_ref[...] = (updated + gate * dot(tri, wfin_ref[...])).astype(BF16)
-    drain(left_all.at[: n - 1], left_sems.at[0])
-    drain(right_main.at[: n - 1], right_sems.at[0])
-    if even:
-        drain(right_tail.at[: n - 1], tail_sems.at[0])
-    else:
-        drain(right_tail.at[: nz - 1], tail_sems.at[0], full)
-        drain(right_tail.at[:nz], tail_sems.at[0], short)
+    out_ref[...] = (updated_buf[...] + gate_buf[...] * dot(tri, wfin_ref[...])).astype(BF16)
+    for b in range(nb):
+        size = most if even or b == wide else least
+        drain(right_all.at[: nz - 1, :size], right_sems.at[0])
+        drain(right_all.at[:1, :size], right_sems.at[0], branch != b)
+    drain(left_all.at[: n - 1], pass_sems.at[0])
     drain(flag_all.at[: n - 1], flag_sems.at[0])
     if redo:
-        drain(left_last.at[:1], last_sems.at[0], dap == 0)
-        drain(left_last.at[:nb], last_sems.at[0], dap != 0)
+        drain(left_last.at[0], last_sems.at[0], dap != 0)
+        drain(left_last.at[:nz], last_sems.at[2], dap == 0)
         drain(base_send, base_sems.at[0], dap == end)
     for fewer, last in ((1, redo & (dap == end)), (0, ~(redo & (dap == end)))):
         if even:
@@ -459,14 +490,13 @@
             dma((OPERANDS,)),
             pltpu.VMEM((n, 1, LANES), F32),
             pltpu.VMEM((nb, groups, seqs, LANES), BF16),
-            pltpu.VMEM((n, groups - 1, seqs, LANES), BF16),
-            pltpu.VMEM((n, seqs, LANES), BF16),
+            pltpu.VMEM((n, groups, seqs, LANES), BF16),
             pltpu.VMEM((nz, nb, seqs, LANES), BF16),
             pltpu.VMEM((n, nb, seqs, LANES), BF16),
             pltpu.VMEM((n, nb, seqs, LANES), BF16),
             pltpu.VMEM((nz, slots, width), BF16),
-            pltpu.VMEM((seqs * amino, LANES), F32),
-            pltpu.VMEM((groups, nb * LANES, LANES), F32),
+            pltpu.VMEM((seqs * (amino + 1), LANES), F32),
+            pltpu.VMEM((groups, nb * rows * (inner + 1), LANES), F32),
             pltpu.VMEM((nb, rows * amino, width), F32),
             pltpu.VMEM((slots, width), BF16),
             pltpu.VMEM((slots, width), BF16),
@@ -477,10 +507,12 @@
             pltpu.VMEM((nz, rows, SUB, width), F32),
             pltpu.VMEM((nz, rows, SUB, width), F32),
             pltpu.VMEM((rows * amino, width), F32),
+            pltpu.VMEM((rows * amino, width), F32),
+            pltpu.VMEM((rows * amino, width), F32),
         ]
-        + [dma((2,))] * 6
-        + [dma((1,)), dma((nz,)), dma((1,)), dma((nz,)), dma((3,)), dma((3,))]
-        + [pltpu.SemaphoreType.REGULAR((nz,))],
+        + [dma((2,)), dma((2,)), dma((2,)), dma((4,)), dma((2,)), dma((nz,))]
+        + [dma((1,)), dma((nz,)), dma((1,)), dma((1,)), dma((3,)), dma((3,))]
+        + [pltpu.SemaphoreType.REGULAR((nz - 1,))],
         compiler_params=pltpu.CompilerParams(collective_id=0, has_side_effects=True),
     )(*operands)
     return out.reshape(rows, amino, width)

time: 15.4 us -> 14.7 us (0.955)
  the two profiles are of different devices: /device:TPU:1 before, /device:TPU:0 now
where the time goes in v3:
time: 14.7 us; the launch traced here: 14.5 us
  Pallas kernels  13.9 us (95%)
  local copies, waits for them, and re-layouts  0.62 us (4%)
    pallas_call x1, Pallas kernels, on_device(): pl.pallas_call(functools.partial(kernel, nb, nz), out_shape=pltpu.VMEM((r...  13.9 us
    unnamed x1, local copies, waits for them, and re-layouts  0.62 us

profile of v3, /device:TPU:0, one launch (start us, length us, event | category | flops | bytes accessed | tf_op | source)
XLA Modules:
  0.0 14.5 jit_solution(18015812259772491752)
XLA Ops:
  0.0 13.9 %shard_map.145 = bf16[128,128]{1,0:T(8,128)(2,1)S(1)} custom-call(bf16[512,256]{1,0:T(8,128)(2,1)} %bitcast.11, s32[1,16]{1,0:T(1,128)} %bitcast.16, s32[1,32]{1,0:T(1,128)} %bitcast.17, s32[4,32]{1,0:T(4,128)} %refs_3_.1, bf16[128,128]{1,0:T(8,128)(2,1)} %bitcast.12, f32[1,256]{1,0:T(1,128)} %bitcast.15, bf16[32,256]{1,0:T(8,128)(2,1)} %bitcast.13, ...), custom_call_target="tpu_custom_call" | custom-call | tf_op jit(solution)/shard_map/pallas_call | solution.py:483
  13.9 0.6 %copy.17 = bf16[4,32,128]{2,1,0:T(8,128)(2,1)} copy(bf16[4,32,128]{2,1,0:T(8,128)(2,1)S(1)} %bitcast.10) | data formatting | bytes 65536

commit v4 on v3

--- a/solution.py
+++ b/solution.py
@@ -85,14 +85,6 @@
     def target(peer):
         return {"branch": peer[0], "dap": peer[1]}
 
-    barrier = pltpu.get_barrier_semaphore()
-    pl.semaphore_signal(barrier, inc=1, device_id=target(partner), device_id_type=MESH)
-    for b, z in everyone[1:]:
-
-        @pl.when(z > dap)
-        def _():
-            pl.semaphore_signal(barrier, inc=1, device_id=target((b, z)), device_id_type=MESH)
-
     loads = {}
     for k in (2,1,0,5,6,7,8,3,4,9,10,11,12,13,14):
         place = held[k].at[branch] if k in (3, 4) else held[k]
@@ -104,6 +96,14 @@
                 pltpu.make_async_copy(operands[0].at[piece], x_ref.at[piece], in_sem.at[0]).start()
         else:
             loads[k].start()
+
+    barrier = pltpu.get_barrier_semaphore()
+    pl.semaphore_signal(barrier, inc=1, device_id=target(partner), device_id_type=MESH)
+    for b, z in everyone[1:]:
+
+        @pl.when(z > dap)
+        def _():
+            pl.semaphore_signal(barrier, inc=1, device_id=target((b, z)), device_id_type=MESH)
 
     pl.semaphore_wait(barrier, dap * nb + 1)
     for b, z in everyone[1:]:
@@ -151,13 +151,44 @@
 
     for k in (0, 5, 6, 7):
         loads[k].wait()
-    normed = standardize(x_ref[...].astype(F32), hgain_ref[...]).astype(BF16)
+    depth = x_ref.shape[1]
+    mean = dot(x_ref[...], jnp.ones((depth, LANES), BF16)) * (1.0 / depth)
+    centred = x_ref[...].astype(F32) - jnp.concatenate([mean] * (depth // LANES), axis=1)
+    spread = jnp.mean(centred * centred, axis=-1, keepdims=True)
+    normed = (centred * lax.rsqrt(spread + 1e-05) * hgain_ref[...]).astype(BF16)
     w_both = jnp.concatenate([wl_ref[...]] * reps + [wr_ref[...]] * reps, axis=0)
     sides = lax.dot_general(
         normed, w_both, (((1,), (1,)), ((), ())), preferred_element_type=F32
     )
     for i in range(seqs):
         y_left[pl.ds(i * (amino + 1), amino), :] = sides[i * amino : (i + 1) * amino, :LANES]
+    for d in range(n):
+        block = y_left[pl.ds(d * rows, seqs, stride=amino + 1), :]
+        for g in range(1, rows):
+            block = jnp.where(
+                lane_group == g, y_left[pl.ds(d * rows + g, seqs, stride=amino + 1), :], block
+            )
+        left_send[d % nz, d // nz] = (block * alane[:, d * LANES : (d + 1) * LANES]).astype(BF16)
+
+    def guarded(when, act):
+        if when is None:
+            act()
+        else:
+            pl.when(when)(act)
+
+    def push(src, dst, ssem, rsem, peer, when=None):
+        copy = pltpu.make_async_remote_copy(
+            src_ref=src, dst_ref=dst, send_sem=ssem, recv_sem=rsem,
+            device_id=target(peer), device_id_type=MESH,
+        )
+        guarded(when, copy.start)
+
+    def push_left(z):
+        push(left_send.at[z], left_all.at[me], pass_sems.at[0], left_rsem.at[dap], (branch, z))
+
+    first_left = order[:1]
+    for z in first_left:
+        pl.when(z < dap)(functools.partial(push_left, z))
     right_rows = [
         dot(gather, sides[h * span : (h + 1) * span, LANES:].astype(BF16)) for h, gather in enumerate(gather_right)
     ]
@@ -172,27 +203,6 @@
             for g in range(1, reps):
                 block = jnp.where(lane_group == g, right_of(begin + g), block)
             right_send[b, t] = block.astype(BF16)
-    for d in range(n):
-        block = y_left[pl.ds(d * rows, seqs, stride=amino + 1), :]
-        for g in range(1, rows):
-            block = jnp.where(
-                lane_group == g, y_left[pl.ds(d * rows + g, seqs, stride=amino + 1), :], block
-            )
-        left_send[d % nz, d // nz] = (block * alane[:, d * LANES : (d + 1) * LANES]).astype(BF16)
-
-
-    def push(src, dst, ssem, rsem, peer, when=None):
-        copy = pltpu.make_async_remote_copy(
-            src_ref=src, dst_ref=dst, send_sem=ssem, recv_sem=rsem,
-            device_id=target(peer), device_id_type=MESH,
-        )
-        guarded(when, copy.start)
-
-    def guarded(when, act):
-        if when is None:
-            act()
-        else:
-            pl.when(when)(act)
 
     def drain(ref, ssem, when=None):
         wait = pltpu.make_async_remote_copy(
@@ -217,16 +227,16 @@
             right_send.at[b, :size], right_all.at[me, :size], right_sems.at[0], right_sems.at[1], (b, z), when
         )
 
-    def push_left(z):
-        push(left_send.at[z], left_all.at[me], pass_sems.at[0], left_rsem.at[dap], (branch, z))
-
-    for z in order:
+    for k, z in enumerate(order):
 
         @pl.when(z > dap)
         def _():
             pl.semaphore_wait(ready.at[z - 1], nb)
 
-        push_left(z)
+        if k < len(first_left):
+            pl.when(z > dap)(functools.partial(push_left, z))
+        else:
+            push_left(z)
         if redo:
             push(left_send.at[end], left_last.at[me], last_sems.at[0], last_sems.at[1], (branch, 0), z == 0)
         for b in range(nb):

time: 14.7 us -> 14.8 us (level)
  no operation moved by 1% of the time
where the time goes in v4:
time: 14.8 us; the launch traced here: 14.5 us
  Pallas kernels  13.9 us (94%)
  local copies, waits for them, and re-layouts  0.62 us (4%)
    pallas_call x1, Pallas kernels, on_device(): pl.pallas_call(functools.partial(kernel, nb, nz), out_shape=pltpu.VMEM((r...  13.9 us
    unnamed x1, local copies, waits for them, and re-layouts  0.62 us

profile of v4, /device:TPU:0, one launch (start us, length us, event | category | flops | bytes accessed | tf_op | source)
XLA Modules:
  0.0 14.5 jit_solution(10695569456246649218)
XLA Ops:
  0.0 13.9 %shard_map.145 = bf16[128,128]{1,0:T(8,128)(2,1)S(1)} custom-call(bf16[512,256]{1,0:T(8,128)(2,1)} %bitcast.11, s32[1,16]{1,0:T(1,128)} %bitcast.16, s32[1,32]{1,0:T(1,128)} %bitcast.17, s32[4,32]{1,0:T(4,128)} %refs_3_.1, bf16[128,128]{1,0:T(8,128)(2,1)} %bitcast.12, f32[1,256]{1,0:T(1,128)} %bitcast.15, bf16[32,256]{1,0:T(8,128)(2,1)} %bitcast.13, ...), custom_call_target="tpu_custom_call" | custom-call | tf_op jit(solution)/shard_map/pallas_call | solution.py:493
  13.9 0.6 %copy.17 = bf16[4,32,128]{2,1,0:T(8,128)(2,1)} copy(bf16[4,32,128]{2,1,0:T(8,128)(2,1)S(1)} %bitcast.10) | data formatting | bytes 65536

commit v5 on v4

--- a/solution.py
+++ b/solution.py
@@ -11,6 +11,7 @@
 BF16 = jnp.bfloat16
 MESH = pl.DeviceIdType.MESH
 OPERANDS = 15
+HELD = 11
 LANES = 128
 SUB = 8
 
@@ -34,10 +35,9 @@
     nb, nz,
     *refs,
 ):
-    operands, out_ref, held = refs[:OPERANDS], refs[OPERANDS], refs[OPERANDS + 1 : 2 * OPERANDS + 1]
-    in_sem, *scratch = refs[2 * OPERANDS + 1 :]
-    (x_ref, hflag_ref, aflag_ref, class_all, couple_all, hgain_ref, wl_ref, wr_ref, wout_ref,
-     embed_ref, cgain_ref, wedge_ref, wgate_ref, wfin_ref, tgain_ref) = held
+    operands, out_ref, held = refs[:OPERANDS], refs[OPERANDS], refs[OPERANDS + 1 : OPERANDS + 1 + HELD]
+    in_sem, *scratch = refs[OPERANDS + 1 + HELD :]
+    x_ref, hflag_ref, aflag_ref, class_all, couple_all, hgain_ref, side_ref, tall_ref, embed_ref, gain_ref, wedge_ref = held
     (
     flag_all, right_send, right_all, left_send, left_all, left_last, tri_all, y_left, outer_buf,
     base_buf, base_send, base_last, product_all, edge_buf, spread_buf, own_buf, part_send, part_in, tri_buf, updated_buf, gate_buf,
@@ -51,7 +51,7 @@
     amino = aflag_ref.shape[1]
     seqs = hflag_ref.shape[1]
     rows = class_all.shape[1]
-    inner = wl_ref.shape[0]
+    inner = side_ref.shape[1]
     width = couple_all.shape[2]
     reps = LANES // inner
     live = amino - 3 * amino // 8
@@ -79,23 +79,37 @@
     partner = (other, dap)
     everyone = [partner] + [(b, z) for z in chips for b in (branch, other)]
 
+    def rank_at(z):
+        return dap - (dap > z)
+
     def index_of(peer):
         return peer[0] * nz + peer[1]
 
     def target(peer):
         return {"branch": peer[0], "dap": peer[1]}
 
-    loads = {}
-    for k in (2,1,0,5,6,7,8,3,4,9,10,11,12,13,14):
-        place = held[k].at[branch] if k in (3, 4) else held[k]
-        loads[k] = pltpu.make_async_copy(operands[k], place, in_sem.at[k])
-        if k == 0:
-            step = x_ref.shape[0] // 8
-            for j in range(8):
-                piece = pl.ds(j * step, step)
-                pltpu.make_async_copy(operands[0].at[piece], x_ref.at[piece], in_sem.at[0]).start()
-        else:
-            loads[k].start()
+    long = inner * inner
+    homes = [
+        (x_ref, 0), (hflag_ref, 1), (aflag_ref, 2), (class_all.at[branch], 3), (couple_all.at[branch], 4),
+        (hgain_ref, 5), (side_ref.at[0], 6), (side_ref.at[1], 6), (tall_ref.at[:long], 7), (embed_ref, 8),
+        (gain_ref.at[0], 9), (wedge_ref, 10), (tall_ref.at[long : long + width], 7),
+        (tall_ref.at[long + width :], 7), (gain_ref.at[1], 9),
+    ]
+    whole_homes = {6: side_ref, 7: tall_ref, 9: gain_ref}
+    for k in (2, 1, 0, 5, 6, 7, 8, 3, 4, 9, 10, 11, 12, 13, 14):
+        home, sem = homes[k]
+        pieces = 8 if k == 0 else 1
+        for p in range(pieces):
+            step = home.shape[0] // pieces
+            source, target_ref = operands[k], home
+            if pieces > 1:
+                source, target_ref = source.at[pl.ds(p * step, step)], target_ref.at[pl.ds(p * step, step)]
+            pltpu.make_async_copy(source, target_ref, in_sem.at[sem]).start()
+
+    def loaded(*keys):
+        for sem in sorted({homes[k][1] for k in keys}):
+            ref = whole_homes[sem] if sem in whole_homes else next(home for home, at in homes if at == sem)
+            pltpu.make_async_copy(ref, ref, in_sem.at[sem]).wait()
 
     barrier = pltpu.get_barrier_semaphore()
     pl.semaphore_signal(barrier, inc=1, device_id=target(partner), device_id_type=MESH)
@@ -119,8 +133,7 @@
             right_all[:, least:] = jnp.zeros((n, most - least, seqs, LANES), BF16)
             tri_all[:, firm:, :] = jnp.zeros((nz, slots - firm, width), BF16)
 
-    loads[2].wait()
-    loads[1].wait()
+    loaded(2, 1)
     aflag = jnp.broadcast_to(aflag_ref[...].astype(F32), (SUB, amino)).astype(BF16)
     hflag32 = hflag_ref[...].astype(F32)
     hflag = jnp.broadcast_to(hflag32, (SUB, seqs)).astype(BF16)
@@ -149,14 +162,13 @@
         (iota((amino, amino * inner), 0) == iota((amino, amino * inner), 1) // inner).astype(BF16),
     )[0:1, :]
 
-    for k in (0, 5, 6, 7):
-        loads[k].wait()
+    loaded(0, 5, 6, 7)
     depth = x_ref.shape[1]
     mean = dot(x_ref[...], jnp.ones((depth, LANES), BF16)) * (1.0 / depth)
     centred = x_ref[...].astype(F32) - jnp.concatenate([mean] * (depth // LANES), axis=1)
     spread = jnp.mean(centred * centred, axis=-1, keepdims=True)
     normed = (centred * lax.rsqrt(spread + 1e-05) * hgain_ref[...]).astype(BF16)
-    w_both = jnp.concatenate([wl_ref[...]] * reps + [wr_ref[...]] * reps, axis=0)
+    w_both = jnp.concatenate([side_ref[0]] * reps + [side_ref[1]] * reps, axis=0)
     sides = lax.dot_general(
         normed, w_both, (((1,), (1,)), ((), ())), preferred_element_type=F32
     )
@@ -184,7 +196,7 @@
         guarded(when, copy.start)
 
     def push_left(z):
-        push(left_send.at[z], left_all.at[me], pass_sems.at[0], left_rsem.at[dap], (branch, z))
+        push(left_send.at[z], left_all.at[me], pass_sems.at[0], left_rsem.at[rank_at(z)], (branch, z))
 
     first_left = order[:1]
     for z in first_left:
@@ -247,8 +259,7 @@
         push_right(b, dap, branch != b)
     push(left_send.at[dap], left_all.at[me], pass_sems.at[0], pass_sems.at[1], partner)
     push(flag_all.at[me], flag_all.at[me], flag_sems.at[0], flag_sems.at[1], partner)
-    for k in (3, 4):
-        loads[k].wait()
+    loaded(3, 4)
     share(class_all, 0)
     share(couple_all, 1)
     left_all[me] = left_send[dap]
@@ -265,8 +276,7 @@
         def _():
             left_last[me] = left_send[end]
 
-    for k in (8, 9, 10, 11, 12, 13, 14):
-        loads[k].wait()
+    loaded(8, 9, 10, 11)
     chip_pairs = nb * pairs
     lane_pair = iota((1, chip_pairs), 1)
     key_pair = lane_keys(chip_pairs)
@@ -316,7 +326,7 @@
 
     for z in chips:
         d = branch * nz + z
-        arrived(left_all.at[d], left_rsem.at[z])
+        arrived(left_all.at[d], left_rsem.at[z - (z > dap)])
         push(left_all.at[d], left_all.at[d], pass_sems.at[0], pass_sems.at[1], partner)
     if redo:
         arrived(left_last.at[: nz - 1], last_sems.at[1], dap == 0)
@@ -355,15 +365,20 @@
                             continue
                         b = a | span
                         shift = span * inner
-                        new[a] = jnp.where(upper, pltpu.roll(block[b], shift, 1), block[a])
-                        new[b] = jnp.where(upper, block[b], pltpu.roll(block[a], LANES - shift, 1))
+                        if 2 * shift == LANES:
+                            moved = pltpu.roll(jnp.where(upper, block[a], block[b]), shift, 1)
+                            new[a] = jnp.where(upper, moved, block[a])
+                            new[b] = jnp.where(upper, block[b], moved)
+                        else:
+                            new[a] = jnp.where(upper, pltpu.roll(block[b], shift, 1), block[a])
+                            new[b] = jnp.where(upper, block[b], pltpu.roll(block[a], LANES - shift, 1))
                     block = new
                     span //= 2
                 for g in range(reps):
                     parts[t * reps + g].append(block[g])
         packed = jnp.concatenate([jnp.concatenate(p, axis=1) for p in parts], axis=0).astype(BF16)
-        product = dot(packed, wout_ref[...]) / number
-        pair_c = standardize(base + product, cgain_ref[...]).astype(BF16)
+        product = dot(packed, tall_ref[:long]) / number
+        pair_c = standardize(base + product, gain_ref[0]).astype(BF16)
         right_two = dot(pair_c, wedge_ref[:, 2 * width :])
         tri_right = jax.nn.sigmoid(right_two[:, :width]) * right_two[:, width:]
         return product, pair_c, tri_right.astype(BF16)
@@ -378,11 +393,11 @@
     for z in chips:
         skip = redo & (dap == end) & (z == 0)
         if even:
-            push(tri_all.at[dap], tri_all.at[dap], tri_ssem.at[0], tri_rsem.at[dap], (branch, z), ~skip)
+            push(tri_all.at[dap], tri_all.at[dap], tri_ssem.at[0], tri_rsem.at[rank_at(z)], (branch, z), ~skip)
         else:
             for size, when in ((slots, full), (firm, short)):
                 push(
-                    tri_block(dap, size), tri_block(dap, size), tri_ssem.at[0], tri_rsem.at[dap], (branch, z),
+                    tri_block(dap, size), tri_block(dap, size), tri_ssem.at[0], tri_rsem.at[rank_at(z)], (branch, z),
                     when & ~skip,
                 )
 
@@ -429,9 +444,9 @@
         high = whole.astype(BF16)
         rest = (whole - high.astype(F32)).astype(BF16)
         updated = base_buf[branch] + dot(expand, jnp.concatenate([high, rest], axis=0))
-        pair = standardize(updated, cgain_ref[...]).astype(BF16)
+        pair = standardize(updated, gain_ref[0]).astype(BF16)
         updated_buf[...] = updated
-        gate_buf[...] = jax.nn.sigmoid(dot(pair, wgate_ref[...]))
+        gate_buf[...] = jax.nn.sigmoid(dot(pair, tall_ref[long : long + width]))
 
     pl.when(dap != 0)(refresh)
     late = [jnp.where(dap == 0, k + 1, (k + 1 + (k + 1 >= dap)) % nz) for k in range(nz - 1)]
@@ -442,17 +457,17 @@
         @pl.when(~skip)
         def _():
             if even:
-                arrived(tri_all.at[z], tri_rsem.at[z])
+                arrived(tri_all.at[z], tri_rsem.at[z - (z > dap)])
             else:
-                arrived(tri_block(z, slots), tri_rsem.at[z], full)
-                arrived(tri_block(z, firm), tri_rsem.at[z], short)
+                arrived(tri_block(z, slots), tri_rsem.at[z - (z > dap)], full)
+                arrived(tri_block(z, firm), tri_rsem.at[z - (z > dap)], short)
             contribute(z)
     pl.when(dap == 0)(refresh)
     arrived(part_in, part_rsem.at[0])
     for z in range(nz):
         settle(z)
-    tri = standardize(tri_buf[...], tgain_ref[...]).astype(BF16)
-    out_ref[...] = (updated_buf[...] + gate_buf[...] * dot(tri, wfin_ref[...])).astype(BF16)
+    tri = standardize(tri_buf[...], gain_ref[1]).astype(BF16)
+    out_ref[...] = (updated_buf[...] + gate_buf[...] * dot(tri, tall_ref[long + width :])).astype(BF16)
     for b in range(nb):
         size = most if even or b == wide else least
         drain(right_all.at[: nz - 1, :size], right_sems.at[0])
@@ -489,7 +504,15 @@
         couple.reshape(rows * amino, width), hgain.reshape(1, depth), wl.T, wr.T, wout, embed,
         cgain.reshape(1, width), wedge, wgate, wfin, tgain.reshape(1, width),
     )
-    held = [pltpu.VMEM((nb, *a.shape) if k in (3, 4) else a.shape, a.dtype) for k, a in enumerate(operands)]
+    shapes = [a.shape for a in operands]
+    shapes[3], shapes[4] = (nb, *shapes[3]), (nb, *shapes[4])
+    held = [pltpu.VMEM(shapes[k], operands[k].dtype) for k in range(6)] + [
+        pltpu.VMEM((2, inner, depth), BF16),
+        pltpu.VMEM((inner * inner + 2 * width, width), BF16),
+        pltpu.VMEM(shapes[9], BF16),
+        pltpu.VMEM((2, 1, width), F32),
+        pltpu.VMEM(shapes[11], BF16),
+    ]
     out = pl.pallas_call(
         functools.partial(kernel, nb, nz),
         out_shape=pltpu.VMEM((rows * amino, width), BF16),
@@ -497,7 +520,7 @@
         out_specs=pl.BlockSpec(memory_space=pltpu.VMEM),
         scratch_shapes=held
         + [
-            dma((OPERANDS,)),
+            dma((HELD,)),
             pltpu.VMEM((n, 1, LANES), F32),
             pltpu.VMEM((nb, groups, seqs, LANES), BF16),
             pltpu.VMEM((n, groups, seqs, LANES), BF16),
@@ -520,8 +543,8 @@
             pltpu.VMEM((rows * amino, width), F32),
             pltpu.VMEM((rows * amino, width), F32),
         ]
-        + [dma((2,)), dma((2,)), dma((2,)), dma((4,)), dma((2,)), dma((nz,))]
-        + [dma((1,)), dma((nz,)), dma((1,)), dma((1,)), dma((3,)), dma((3,))]
+        + [dma((2,)), dma((2,)), dma((2,)), dma((4,)), dma((2,)), dma((nz - 1,))]
+        + [dma((1,)), dma((nz - 1,)), dma((1,)), dma((1,)), dma((3,)), dma((3,))]
         + [pltpu.SemaphoreType.REGULAR((nz - 1,))],
         compiler_params=pltpu.CompilerParams(collective_id=0, has_side_effects=True),
     )(*operands)

time: 14.8 us -> 14.7 us (level)
  no operation moved by 1% of the time
where the time goes in v5:
time: 14.7 us; the launch traced here: 14.5 us
  Pallas kernels  13.9 us (95%)
  local copies, waits for them, and re-layouts  0.62 us (4%)
    pallas_call x1, Pallas kernels, on_device(): pl.pallas_call(functools.partial(kernel, nb, nz), out_shape=pltpu.VMEM((r...  13.9 us
    unnamed x1, local copies, waits for them, and re-layouts  0.62 us

profile of v5, /device:TPU:0, one launch (start us, length us, event | category | flops | bytes accessed | tf_op | source)
XLA Modules:
  0.0 14.5 jit_solution(11966716848609295076)
XLA Ops:
  0.0 13.9 %shard_map.145 = bf16[128,128]{1,0:T(8,128)(2,1)S(1)} custom-call(bf16[512,256]{1,0:T(8,128)(2,1)} %bitcast.11, s32[1,16]{1,0:T(1,128)} %bitcast.16, s32[1,32]{1,0:T(1,128)} %bitcast.17, s32[4,32]{1,0:T(4,128)} %refs_3_.1, bf16[128,128]{1,0:T(8,128)(2,1)} %bitcast.12, f32[1,256]{1,0:T(1,128)} %bitcast.15, bf16[32,256]{1,0:T(8,128)(2,1)} %bitcast.13, ...), custom_call_target="tpu_custom_call" | custom-call | tf_op jit(solution)/shard_map/pallas_call | solution.py:516
  13.9 0.6 %copy.17 = bf16[4,32,128]{2,1,0:T(8,128)(2,1)} copy(bf16[4,32,128]{2,1,0:T(8,128)(2,1)S(1)} %bitcast.10) | data formatting | bytes 65536

commit v6 on v5

--- a/solution.py
+++ b/solution.py
@@ -245,16 +245,15 @@
         def _():
             pl.semaphore_wait(ready.at[z - 1], nb)
 
-        if k < len(first_left):
-            pl.when(z > dap)(functools.partial(push_left, z))
-        else:
-            push_left(z)
+        pl.when(z > dap)(functools.partial(push_left, z))
         if redo:
             push(left_send.at[end], left_last.at[me], last_sems.at[0], last_sems.at[1], (branch, 0), z == 0)
         for b in range(nb):
+            push(flag_all.at[me], flag_all.at[me], flag_sems.at[0], flag_sems.at[1], (b, z))
+        for b in range(nb):
             push_right(b, z)
-        for b in range(nb):
-            push(flag_all.at[me], flag_all.at[me], flag_sems.at[0], flag_sems.at[1], (b, z))
+            if b == 0 and k + 1 < len(order):
+                pl.when(order[k + 1] < dap)(functools.partial(push_left, order[k + 1]))
     for b in range(nb):
         push_right(b, dap, branch != b)
     push(left_send.at[dap], left_all.at[me], pass_sems.at[0], pass_sems.at[1], partner)
@@ -449,7 +448,7 @@
         gate_buf[...] = jax.nn.sigmoid(dot(pair, tall_ref[long : long + width]))
 
     pl.when(dap != 0)(refresh)
-    late = [jnp.where(dap == 0, k + 1, (k + 1 + (k + 1 >= dap)) % nz) for k in range(nz - 1)]
+    late = [jnp.where(dap == 0, end - k, (k + 1 + (k + 1 >= dap)) % nz) for k in range(nz - 1)]
     late = [jnp.where((dap == 0) | (k < nz - 2), z, 0) for k, z in enumerate(late)]
     for k, z in enumerate(late):
         skip = redo & (dap == 0) & (z == end)
@@ -466,7 +465,7 @@
     arrived(part_in, part_rsem.at[0])
     for z in range(nz):
         settle(z)
-    tri = standardize(tri_buf[...], gain_ref[1]).astype(BF16)
+    tri = standardize(tri_buf[:pairs], gain_ref[1]).astype(BF16)
     out_ref[...] = (updated_buf[...] + gate_buf[...] * dot(tri, tall_ref[long + width :])).astype(BF16)
     for b in range(nb):
         size = most if even or b == wide else least
@@ -528,8 +527,8 @@
             pltpu.VMEM((n, nb, seqs, LANES), BF16),
             pltpu.VMEM((n, nb, seqs, LANES), BF16),
             pltpu.VMEM((nz, slots, width), BF16),
-            pltpu.VMEM((seqs * (amino + 1), LANES), F32),
-            pltpu.VMEM((groups, nb * rows * (inner + 1), LANES), F32),
+            pltpu.VMEM(((seqs + 1) * (amino + 1), LANES), F32),
+            pltpu.VMEM((groups, (nb * rows + 1) * (inner + 1), LANES), F32),
             pltpu.VMEM((nb, rows * amino, width), F32),
             pltpu.VMEM((slots, width), BF16),
             pltpu.VMEM((slots, width), BF16),
@@ -539,7 +538,7 @@
             pltpu.VMEM((nz, rows, SUB, width), F32),
             pltpu.VMEM((nz, rows, SUB, width), F32),
             pltpu.VMEM((nz, rows, SUB, width), F32),
-            pltpu.VMEM((rows * amino, width), F32),
+            pltpu.VMEM((rows * amino + SUB, width), F32),
             pltpu.VMEM((rows * amino, width), F32),
             pltpu.VMEM((rows * amino, width), F32),
         ]

time: 14.7 us -> 14.5 us (0.986)
  no operation moved by 1% of the time
where the time goes in v6:
time: 14.5 us; the launch traced here: 14.4 us
  Pallas kernels  13.8 us (95%)
  local copies, waits for them, and re-layouts  0.62 us (4%)
    pallas_call x1, Pallas kernels, on_device(): pl.pallas_call(functools.partial(kernel, nb, nz), out_shape=pltpu.VMEM((r...  13.8 us
    unnamed x1, local copies, waits for them, and re-layouts  0.62 us

profile of v6, /device:TPU:0, one launch (start us, length us, event | category | flops | bytes accessed | tf_op | source)
XLA Modules:
  0.0 14.4 jit_solution(14545379309488629587)
XLA Ops:
  0.0 13.8 %shard_map.145 = bf16[128,128]{1,0:T(8,128)(2,1)S(1)} custom-call(bf16[512,256]{1,0:T(8,128)(2,1)} %bitcast.11, s32[1,16]{1,0:T(1,128)} %bitcast.16, s32[1,32]{1,0:T(1,128)} %bitcast.17, s32[4,32]{1,0:T(4,128)} %refs_3_.1, bf16[128,128]{1,0:T(8,128)(2,1)} %bitcast.12, f32[1,256]{1,0:T(1,128)} %bitcast.15, bf16[32,256]{1,0:T(8,128)(2,1)} %bitcast.13, ...), custom_call_target="tpu_custom_call" | custom-call | tf_op jit(solution)/shard_map/pallas_call | solution.py:515
  13.8 0.6 %copy.17 = bf16[4,32,128]{2,1,0:T(8,128)(2,1)} copy(bf16[4,32,128]{2,1,0:T(8,128)(2,1)S(1)} %bitcast.10) | data formatting | bytes 65536

commit v7 on v6

--- a/solution.py
+++ b/solution.py
@@ -402,12 +402,14 @@
 
     product_all[branch] = product
     share(product_all, 2)
-    left_two = dot(pair_c, wedge_ref[:, : 2 * width])
-    edge_buf[...] = (jax.nn.sigmoid(left_two[:, :width]) * left_two[:, width:]).astype(BF16).astype(F32)
-    for i in range(block_rows):
-        for k in range(part):
-            row = edge_buf[k * block_rows + i : k * block_rows + i + 1, :]
-            spread_buf[i, k * SUB : (k + 1) * SUB, :] = jnp.broadcast_to(row, (SUB, width))
+
+    def edges():
+        left_two = dot(pair_c, wedge_ref[:, : 2 * width])
+        edge_buf[...] = (jax.nn.sigmoid(left_two[:, :width]) * left_two[:, width:]).astype(BF16).astype(F32)
+        for i in range(block_rows):
+            for k in range(part):
+                row = edge_buf[k * block_rows + i : k * block_rows + i + 1, :]
+                spread_buf[i, k * SUB : (k + 1) * SUB, :] = jnp.broadcast_to(row, (SUB, width))
 
     def triangle(z, side, store):
         block = tri_all[z].astype(F32)
@@ -427,7 +429,9 @@
                 row = i * amino + (b * nz + z) * rows
                 tri_buf[pl.ds(pl.multiple_of(row, rows), rows), :] = total[b * rows : (b + 1) * rows]
 
-    contribute(dap)
+    if not redo:
+        edges()
+        contribute(dap)
     if redo:
 
         @pl.when(dap == 0)
@@ -435,6 +439,13 @@
             arrived(left_last.at[:nz], last_sems.at[3])
             arrived(base_last, base_sems.at[1])
             tri_all[end] = middle(left_last, base_last[...].astype(F32))[2]
+            edges()
+
+        pl.when(dap != 0)(edges)
+        contribute(dap)
+
+        @pl.when(dap == 0)
+        def _():
             contribute(end)
 
     def refresh():

time: 14.5 us -> 14.5 us (level)
  no operation moved by 1% of the time
where the time goes in v7:
time: 14.5 us; the launch traced here: 14.4 us
  Pallas kernels  13.8 us (95%)
  local copies, waits for them, and re-layouts  0.62 us (4%)
    pallas_call x1, Pallas kernels, on_device(): pl.pallas_call(functools.partial(kernel, nb, nz), out_shape=pltpu.VMEM((r...  13.8 us
    unnamed x1, local copies, waits for them, and re-layouts  0.62 us

profile of v7, /device:TPU:0, one launch (start us, length us, event | category | flops | bytes accessed | tf_op | source)
XLA Modules:
  0.0 14.4 jit_solution(12837975619780377302)
XLA Ops:
  0.0 13.8 %shard_map.145 = bf16[128,128]{1,0:T(8,128)(2,1)S(1)} custom-call(bf16[512,256]{1,0:T(8,128)(2,1)} %bitcast.11, s32[1,16]{1,0:T(1,128)} %bitcast.16, s32[1,32]{1,0:T(1,128)} %bitcast.17, s32[4,32]{1,0:T(4,128)} %refs_3_.1, bf16[128,128]{1,0:T(8,128)(2,1)} %bitcast.12, f32[1,256]{1,0:T(1,128)} %bitcast.15, bf16[32,256]{1,0:T(8,128)(2,1)} %bitcast.13, ...), custom_call_target="tpu_custom_call" | custom-call | tf_op jit(solution)/shard_map/pallas_call | solution.py:526
  13.8 0.6 %copy.17 = bf16[4,32,128]{2,1,0:T(8,128)(2,1)} copy(bf16[4,32,128]{2,1,0:T(8,128)(2,1)S(1)} %bitcast.10) | data formatting | bytes 65536
